TPU v7x, 128 devices: a whole 4x4x4 slice. The times are simulated.
128 devices in a mesh: dx: 8 (over z, core), dy: 16 (over x, y).
Axes of the slice: x: 4, y: 4, z: 4, core: 2. Of those that a mesh axis runs over, the one named last changes fastest.
Arguments:
- dust: bfloat16 [524288, 256], P(('dx', 'dy')), may hold values from 0.19921875 to 2
- classes: int32 [524288], P(('dx', 'dy')), may hold values from 0 to 7
- kernels: bfloat16 [8, 2, 128, 128], replicated, may hold values from -0.5 to 0.5
- export_ids: int32 [128, 4, 1024], P(('dx', 'dy')), may hold values from 0 to 4095
- faces: int32 [6, 524288], P(None, ('dx', 'dy')), may hold values from 0 to 8191, as said below
- face_coef: float32 [6, 524288], P(None, ('dx', 'dy')), may hold values from 0.04 to 0.16
- mig_ids: int32 [16384, 16], P(('dx', 'dy')), may hold values from 0 to 4095, as said below
- mig_counts: int32 [128, 128], P(('dx', 'dy')), may hold values from 0 to 16, as said below
Outputs:
- dust_next: bfloat16 [524288, 256], P(('dx', 'dy'))
- arrivals: bfloat16 [262144, 256], P(('dx', 'dy'))
Inputs may be any that keep to these rules, and one draw needn't show every extreme that they name: Entries below 4096 name cells of the same domain, entries from 4096 on name its received rows in the order of the steps; each cell has 4 to 6 faces and its other slots name the cell itself. `mig_ids`: the 2048 entries of one domain's rows are distinct local cells. `mig_counts`: one destination, drawn from the seed, receives 16 cells from every domain.
All inputs are finite; a program needn't handle non-finite values.
Results may differ from a plain program's by a relative error of at most 0.0054.
Values may be sent and summed in bfloat16 or wider, within the bound.
A program may use at most 64 MiB of HBM per device.

v0:
```python
import jax
import jax.numpy as jnp
from jax import lax
from jax.sharding import PartitionSpec as P

SUBSTEPS = 6


def passed_along(block, axis, distance):
    devices = range(lax.axis_size(axis))
    route = [((i - distance) % len(devices), i) for i in devices]
    return lax.ppermute(block, axis, route)


def coagulate(dust_rows, dust_classes, kernels):
    row_count = dust_rows.shape[0]
    class_count = kernels.shape[0]
    species = kernels.shape[1]
    bins = kernels.shape[2]
    block_rows = 2048
    block_count = row_count // block_rows
    class_ids = jnp.arange(class_count, dtype=jnp.int32)

    def run_block(pieces):
        piece_rows, piece_classes = pieces
        selector = (piece_classes[:, None] == class_ids[None, :]).astype(jnp.bfloat16)
        grain_state = piece_rows.astype(jnp.float32).reshape(block_rows, species, bins)
        for substep in range(SUBSTEPS):
            operand = grain_state.astype(jnp.bfloat16)
            spread = operand[:, :, None, :] * selector[:, None, :, None]
            product = jnp.einsum(
                "rskb,ksbc->rsc", spread, kernels, preferred_element_type=jnp.float32
            )
            mean_square = jnp.mean(grain_state * grain_state, axis=2, keepdims=True)
            grain_state = grain_state + product * (mean_square / (1.0 + mean_square))
        return grain_state.reshape(block_rows, species * bins).astype(jnp.bfloat16)

    blocked = lax.map(
        run_block,
        (
            dust_rows.reshape(block_count, block_rows, species * bins),
            dust_classes.reshape(block_count, block_rows),
        ),
    )
    return blocked.reshape(row_count, species * bins)


def body(dust, classes, kernels, export_ids, faces, face_coef, mig_ids, mig_counts):
    row_width = dust.shape[1]
    export_rows = export_ids.reshape(4, export_ids.shape[2])
    export_count = export_rows.shape[1]
    coag = coagulate(dust, classes, kernels)
    outbound = jnp.take(coag, export_rows.reshape(4 * export_count), axis=0).reshape(
        4, export_count, row_width
    )
    received = []
    for direction, offset in ((0, 1), (1, -1)):
        received.append(passed_along(outbound[direction], "dx", offset))
    for direction, offset in ((2, 1), (3, -1)):
        received.append(passed_along(outbound[direction], "dy", offset))
    ghosts = jnp.concatenate(received, axis=0)
    extended = jnp.concatenate([coag, ghosts], axis=0)
    own_rows = coag.astype(jnp.float32)
    flux_sum = own_rows
    for face in range(faces.shape[0]):
        neighbour = jnp.take(extended, faces[face], axis=0).astype(jnp.float32)
        flux_sum = flux_sum + face_coef[face][:, None] * (neighbour - own_rows)
    updated = flux_sum.astype(jnp.bfloat16)
    domains = mig_counts.shape[1]
    capacity = mig_ids.shape[1]
    filled = jnp.arange(capacity, dtype=jnp.int32)[None, :] < mig_counts[0][:, None]
    picked = jnp.take(updated, mig_ids.reshape(domains * capacity), axis=0).reshape(
        domains, capacity, row_width
    )
    leaving = jnp.where(filled[:, :, None], picked, jnp.zeros_like(picked))
    arrived = lax.all_to_all(leaving, ("dx", "dy"), split_axis=0, concat_axis=0, tiled=True)
    arrivals = arrived.reshape(domains * capacity, row_width)
    return (updated, arrivals)


def solution(mesh):
    return jax.shard_map(
        body,
        mesh=mesh,
        in_specs=(
            P(("dx", "dy"), None),
            P(("dx", "dy")),
            P(),
            P(("dx", "dy"), None, None),
            P(None, ("dx", "dy")),
            P(None, ("dx", "dy")),
            P(("dx", "dy"), None),
            P(("dx", "dy"), None),
        ),
        out_specs=(P(("dx", "dy"), None), P(("dx", "dy"), None)),
        check_vma=False,
    )
```

profile of v0, /device:TPU:1, one launch (start us, length us, event | category | flops | bytes accessed | tf_op | source)
XLA Modules:
  0.0 322.1 jit_solution(15725213917221664605)
XLA Ops:
  0.6 2.1 copy.26
  3.4 114.1 %while.11 = (s32[]{:T(128)}, bf16[2,2048,256]{2,1,0:T(8,128)(2,1)S(1)}, bf16[2,2048,256]{2,1,0:T(8,128)(2,1)}, s32[2,2048]{1,0:T(2,128)S(1)}, bf16[8,2,128,128]{2,3,0,1:T(8,128)(2,1)}, /*index=5*/s32[]{:T(128)}) while((s32[]{:T(128)}, bf16[2,2048,256]{2,1,0:T(8,128)(2,1)S(1)}, bf16[2,2048,256]{2,1,0:T(8,128)(2,1)}, ...), condition=%wide.region_7.8_spmd.clone, body=%wide.region_0.7_spmd.clone.sunk | while | flops 6484475904 | bytes 60416080 | solution.py:38
  3.5 2.3 constant_dynamic-slice_fusion.4
  5.7 1.5 copy.52
  8.8 7.0 %multiply_reduce_fusion.10 = (f32[2048,2]{0,1:T(2,128)S(1)}, bf16[2048,2,128]{0,2,1:T(8,128)(2,1)}, f32[2048,2,128]{0,2,1:T(8,128)}) fusion(f32[2048,2]{0,1:T(2,128)S(1)} %add_divide_fusion.12, bf16[8,2,128,128]{2,3,0,1:T(8,128)(2,1)} %get-tuple-element.188, bf16[2048,8]{0,1:T(8,128)(2,1)S(1)} %fusion.130, bf16[2048,2,128]{2,0,1:T(8,128)(2,1)} %copy.53, ...), kind=kOutput, calls=%fused_computation.58.clone.1 | convolution fusion | flops 1081077760 | bytes 5832704 | tf_op jit(solution)/shard_map/while/body/eval_jaxpr/rskb,ksbc->rsc/dot_general | solution.py:31
  15.8 1.6 copy.54
  17.5 7.1 %multiply_reduce_fusion.11 = (f32[2048,2]{0,1:T(2,128)S(1)}, bf16[2048,2,128]{0,2,1:T(8,128)(2,1)}, f32[2048,2,128]{0,2,1:T(8,128)}) fusion(f32[2048,2,128]{0,2,1:T(8,128)} %get-tuple-element.157, f32[2048,2]{0,1:T(2,128)S(1)} %add_divide_fusion.13, bf16[8,2,128,128]{2,3,0,1:T(8,128)(2,1)} %get-tuple-element.188, ...), kind=kOutput, calls=%fused_computation.57.clone.1 | convolution fusion | flops 1080553472 | bytes 6881280 | tf_op jit(solution)/shard_map/while/body/eval_jaxpr/rskb,ksbc->rsc/dot_general | solution.py:31
  24.5 1.6 copy.55
  26.2 7.1 %multiply_reduce_fusion.12 = (f32[2048,2]{0,1:T(2,128)S(1)}, bf16[2048,2,128]{0,2,1:T(8,128)(2,1)}, f32[2048,2,128]{0,2,1:T(8,128)}) fusion(f32[2048,2,128]{0,2,1:T(8,128)} %get-tuple-element.160, f32[2048,2]{0,1:T(2,128)S(1)} %add_divide_fusion.14, bf16[8,2,128,128]{2,3,0,1:T(8,128)(2,1)} %get-tuple-element.188, ...), kind=kOutput, calls=%fused_computation.56.clone.1 | convolution fusion | flops 1080553472 | bytes 6881280 | tf_op jit(solution)/shard_map/while/body/eval_jaxpr/rskb,ksbc->rsc/dot_general | solution.py:31
  33.2 1.6 copy.56
  34.9 7.1 %multiply_reduce_fusion.13 = (f32[2048,2]{0,1:T(2,128)S(1)}, bf16[2048,2,128]{0,2,1:T(8,128)(2,1)}, f32[2048,2,128]{0,2,1:T(8,128)}) fusion(f32[2048,2,128]{0,2,1:T(8,128)} %get-tuple-element.163, f32[2048,2]{0,1:T(2,128)S(1)} %add_divide_fusion.15, bf16[8,2,128,128]{2,3,0,1:T(8,128)(2,1)} %get-tuple-element.188, ...), kind=kOutput, calls=%fused_computation.55.clone.1 | convolution fusion | flops 1080553472 | bytes 6881280 | tf_op jit(solution)/shard_map/while/body/eval_jaxpr/rskb,ksbc->rsc/dot_general | solution.py:31
  41.9 1.6 copy.57
  43.6 7.1 %multiply_reduce_fusion.14 = (f32[2048,2]{0,1:T(2,128)S(1)}, bf16[2048,2,128]{0,2,1:T(8,128)(2,1)}, f32[2048,2,128]{0,2,1:T(8,128)}) fusion(f32[2048,2,128]{0,2,1:T(8,128)} %get-tuple-element.166, f32[2048,2]{0,1:T(2,128)S(1)} %add_divide_fusion.16, bf16[8,2,128,128]{2,3,0,1:T(8,128)(2,1)} %get-tuple-element.188, ...), kind=kOutput, calls=%fused_computation.54.clone.1 | convolution fusion | flops 1080553472 | bytes 6881280 | tf_op jit(solution)/shard_map/while/body/eval_jaxpr/rskb,ksbc->rsc/dot_general | solution.py:31
  50.6 1.6 copy.58
  52.3 6.6 %fusion.131 = bf16[2048,2,128]{0,2,1:T(8,128)(2,1)} fusion(f32[2048,2,128]{0,2,1:T(8,128)} %get-tuple-element.169, bf16[8,2,128,128]{2,3,0,1:T(8,128)(2,1)} %get-tuple-element.188, bf16[2048,2,128]{2,0,1:T(8,128)(2,1)S(1)} %copy.58, bf16[2048,8]{0,1:T(8,128)(2,1)S(1)} %fusion.130, f32[2048,2]{0,1:T(2,128)S(1)} %add_divide_fusion.17), kind=kOutput, calls=%fused_computation.52.clone.1 | convolution fusion | flops 1079508992 | bytes 4767744 | tf_op jit(solution)/shard_map/while/body/eval_jaxpr/rskb,ksbc->rsc/dot_general | solution.py:31
  58.9 1.5 copy.59
  60.5 2.3 constant_dynamic-slice_fusion.4
  62.8 1.5 copy.52
  65.9 7.0 %multiply_reduce_fusion.10 = (f32[2048,2]{0,1:T(2,128)S(1)}, bf16[2048,2,128]{0,2,1:T(8,128)(2,1)}, f32[2048,2,128]{0,2,1:T(8,128)}) fusion(f32[2048,2]{0,1:T(2,128)S(1)} %add_divide_fusion.12, bf16[8,2,128,128]{2,3,0,1:T(8,128)(2,1)} %get-tuple-element.188, bf16[2048,8]{0,1:T(8,128)(2,1)S(1)} %fusion.130, bf16[2048,2,128]{2,0,1:T(8,128)(2,1)} %copy.53, ...), kind=kOutput, calls=%fused_computation.58.clone.1 | convolution fusion | flops 1081077760 | bytes 5832704 | tf_op jit(solution)/shard_map/while/body/eval_jaxpr/rskb,ksbc->rsc/dot_general | solution.py:31
  72.8 1.6 copy.54
  74.5 7.1 %multiply_reduce_fusion.11 = (f32[2048,2]{0,1:T(2,128)S(1)}, bf16[2048,2,128]{0,2,1:T(8,128)(2,1)}, f32[2048,2,128]{0,2,1:T(8,128)}) fusion(f32[2048,2,128]{0,2,1:T(8,128)} %get-tuple-element.157, f32[2048,2]{0,1:T(2,128)S(1)} %add_divide_fusion.13, bf16[8,2,128,128]{2,3,0,1:T(8,128)(2,1)} %get-tuple-element.188, ...), kind=kOutput, calls=%fused_computation.57.clone.1 | convolution fusion | flops 1080553472 | bytes 6881280 | tf_op jit(solution)/shard_map/while/body/eval_jaxpr/rskb,ksbc->rsc/dot_general | solution.py:31
  81.6 1.6 copy.55
  83.2 7.1 %multiply_reduce_fusion.12 = (f32[2048,2]{0,1:T(2,128)S(1)}, bf16[2048,2,128]{0,2,1:T(8,128)(2,1)}, f32[2048,2,128]{0,2,1:T(8,128)}) fusion(f32[2048,2,128]{0,2,1:T(8,128)} %get-tuple-element.160, f32[2048,2]{0,1:T(2,128)S(1)} %add_divide_fusion.14, bf16[8,2,128,128]{2,3,0,1:T(8,128)(2,1)} %get-tuple-element.188, ...), kind=kOutput, calls=%fused_computation.56.clone.1 | convolution fusion | flops 1080553472 | bytes 6881280 | tf_op jit(solution)/shard_map/while/body/eval_jaxpr/rskb,ksbc->rsc/dot_general | solution.py:31
  90.3 1.6 copy.56
  91.9 7.1 %multiply_reduce_fusion.13 = (f32[2048,2]{0,1:T(2,128)S(1)}, bf16[2048,2,128]{0,2,1:T(8,128)(2,1)}, f32[2048,2,128]{0,2,1:T(8,128)}) fusion(f32[2048,2,128]{0,2,1:T(8,128)} %get-tuple-element.163, f32[2048,2]{0,1:T(2,128)S(1)} %add_divide_fusion.15, bf16[8,2,128,128]{2,3,0,1:T(8,128)(2,1)} %get-tuple-element.188, ...), kind=kOutput, calls=%fused_computation.55.clone.1 | convolution fusion | flops 1080553472 | bytes 6881280 | tf_op jit(solution)/shard_map/while/body/eval_jaxpr/rskb,ksbc->rsc/dot_general | solution.py:31
  99.0 1.6 copy.57
  100.6 7.1 %multiply_reduce_fusion.14 = (f32[2048,2]{0,1:T(2,128)S(1)}, bf16[2048,2,128]{0,2,1:T(8,128)(2,1)}, f32[2048,2,128]{0,2,1:T(8,128)}) fusion(f32[2048,2,128]{0,2,1:T(8,128)} %get-tuple-element.166, f32[2048,2]{0,1:T(2,128)S(1)} %add_divide_fusion.16, bf16[8,2,128,128]{2,3,0,1:T(8,128)(2,1)} %get-tuple-element.188, ...), kind=kOutput, calls=%fused_computation.54.clone.1 | convolution fusion | flops 1080553472 | bytes 6881280 | tf_op jit(solution)/shard_map/while/body/eval_jaxpr/rskb,ksbc->rsc/dot_general | solution.py:31
  107.7 1.6 copy.58
  109.3 6.6 %fusion.131 = bf16[2048,2,128]{0,2,1:T(8,128)(2,1)} fusion(f32[2048,2,128]{0,2,1:T(8,128)} %get-tuple-element.169, bf16[8,2,128,128]{2,3,0,1:T(8,128)(2,1)} %get-tuple-element.188, bf16[2048,2,128]{2,0,1:T(8,128)(2,1)S(1)} %copy.58, bf16[2048,8]{0,1:T(8,128)(2,1)S(1)} %fusion.130, f32[2048,2]{0,1:T(2,128)S(1)} %add_divide_fusion.17), kind=kOutput, calls=%fused_computation.52.clone.1 | convolution fusion | flops 1079508992 | bytes 4767744 | tf_op jit(solution)/shard_map/while/body/eval_jaxpr/rskb,ksbc->rsc/dot_general | solution.py:31
  115.9 1.5 copy.59
  117.6 17.0 %gather_fusion = bf16[4096,256]{1,0:T(8,128)(2,1)} fusion(bf16[4096,256]{1,0:T(8,128)(2,1)S(1)} %bitcast.116, s32[4096]{0:T(1024)S(1)} %broadcast_clamp_fusion), kind=kCustom, calls=%fused_computation.6 | custom fusion | bytes 4210688 | tf_op jit(solution)/shard_map/jit(_take)/gather | solution.py:53
  134.7 1.9 broadcast_select_fusion
  136.6 1.4 fusion.103
  138.0 3.0 collective-permute-start
  142.3 3.9 %collective-permute-start.3 = (bf16[1024,256]{1,0:T(8,128)(2,1)}, bf16[1024,256]{1,0:T(8,128)(2,1)S(1)}, u32[]{:S(2)}, u32[]{:S(2)}) collective-permute-start(bf16[1024,256]{1,0:T(8,128)(2,1)} %get-tuple-element.83), channel_id=1, source_target_pairs={{1,0},{2,1},{3,2},{4,3},{5,4},{6,5},{7,6},{8,7},{9,8},{10,9},{11,1... | collective-permute-start | bytes 1572872 | tf_op jit(solution)/shard_map/ppermute | solution.py:12
  146.2 1.5 constant_dynamic-update-slice_fusion.5
  148.5 1.9 constant_dynamic-update-slice_fusion.4
  150.4 1.9 constant_dynamic-update-slice_fusion.3
  152.3 4.0 %collective-permute-done.2 = bf16[1024,256]{1,0:T(8,128)(2,1)S(1)} collective-permute-done((bf16[1024,256]{1,0:T(8,128)(2,1)}, bf16[1024,256]{1,0:T(8,128)(2,1)S(1)}, u32[]{:S(2)}, u32[]{:S(2)}) %collective-permute-start.2) | collective-permute-done | bytes 524320 | tf_op jit(solution)/shard_map/ppermute | solution.py:12
  157.9 18.7 %gather_fusion.4 = bf16[4096,256]{1,0:T(8,128)(2,1)} fusion(bf16[8192,256]{1,0:T(8,128)(2,1)} %constant_dynamic-update-slice_fusion.1, s32[4096]{0:T(1024)S(1)} %get-tuple-element.101), kind=kCustom, calls=%fused_computation.2.clone | custom fusion | bytes 4210688 | tf_op jit(solution)/shard_map/jit(_take)/gather | solution.py:66
  176.6 18.6 %gather_fusion.5 = bf16[4096,256]{1,0:T(8,128)(2,1)} fusion(bf16[8192,256]{1,0:T(8,128)(2,1)} %constant_dynamic-update-slice_fusion.1, s32[4096]{0:T(1024)S(1)} %get-tuple-element.102), kind=kCustom, calls=%fused_computation.3.clone | custom fusion | bytes 4210688 | tf_op jit(solution)/shard_map/jit(_take)/gather | solution.py:66
  195.2 18.7 %gather_fusion.6 = bf16[4096,256]{1,0:T(8,128)(2,1)} fusion(bf16[8192,256]{1,0:T(8,128)(2,1)} %constant_dynamic-update-slice_fusion.1, s32[4096]{0:T(1024)S(1)} %get-tuple-element.103), kind=kCustom, calls=%fused_computation.4.clone | custom fusion | bytes 4210688 | tf_op jit(solution)/shard_map/jit(_take)/gather | solution.py:66
  213.9 18.7 %gather_fusion.2 = bf16[4096,256]{1,0:T(8,128)(2,1)} fusion(bf16[8192,256]{1,0:T(8,128)(2,1)} %constant_dynamic-update-slice_fusion.1, s32[4096]{0:T(1024)S(1)} %get-tuple-element.99), kind=kCustom, calls=%fused_computation.clone | custom fusion | bytes 4210688 | tf_op jit(solution)/shard_map/jit(_take)/gather | solution.py:66
  232.6 18.7 %gather_fusion.3 = bf16[4096,256]{1,0:T(8,128)(2,1)} fusion(bf16[8192,256]{1,0:T(8,128)(2,1)} %constant_dynamic-update-slice_fusion.1, s32[4096]{0:T(1024)S(1)} %get-tuple-element.100), kind=kCustom, calls=%fused_computation.1.clone | custom fusion | bytes 4210688 | tf_op jit(solution)/shard_map/jit(_take)/gather | solution.py:66
  251.3 18.7 %gather_fusion.7 = bf16[4096,256]{1,0:T(8,128)(2,1)} fusion(bf16[8192,256]{1,0:T(8,128)(2,1)} %constant_dynamic-update-slice_fusion.1, s32[4096]{0:T(1024)S(1)} %get-tuple-element.104), kind=kCustom, calls=%fused_computation.5.clone | custom fusion | bytes 4210688 | tf_op jit(solution)/shard_map/jit(_take)/gather | solution.py:66
  269.9 12.3 %fusion.91 = bf16[4096,256]{1,0:T(8,128)(2,1)} fusion(bf16[4096,256]{1,0:T(8,128)(2,1)} %gather_fusion.7, bf16[4096,256]{1,0:T(8,128)(2,1)} %gather_fusion.6, bf16[4096,256]{1,0:T(8,128)(2,1)} %gather_fusion.5, bf16[4096,256]{1,0:T(8,128)(2,1)} %gather_fusion.4, bf16[4096,256]{1,0:T(8,128)(2,1)} %gather_fusion.3, bf16[4096,256]{1,0:T(8,128)(2,1)} %gather_fusion.2, ...), kind=kLoop, calls=%fused_computation.83 | loop fusion | flops 33554432 | bytes 16900096 | tf_op jit(solution)/shard_map/convert_element_type | solution.py:68
  282.2 8.5 %gather_fusion.1 = bf16[2048,256]{1,0:T(8,128)(2,1)S(1)} fusion(bf16[4096,256]{1,0:T(8,128)(2,1)} %fusion.91, s32[2048]{0:T(1024)S(1)} %broadcast_clamp_fusion.1), kind=kCustom, calls=%fused_computation.7 | custom fusion | bytes 2105344 | tf_op jit(solution)/shard_map/jit(_take)/gather | solution.py:72
  291.5 29.6 %all_to_all.5 = bf16[128,16,256]{2,1,0:T(8,128)(2,1)S(1)} all-to-all(bf16[128,16,256]{2,1,0:T(8,128)(2,1)S(1)} %select_select_fusion), channel_id=1, replica_groups=mesh['dx'=8,'dy'=16] {'dx','dy'}, dimensions={0} | all-to-all | bytes 2097152 | tf_op jit(solution)/shard_map/all_to_all | solution.py:76
  (62 shorter events, 9.7 us)
Async XLA Ops:
  3.4 114.1 %copy-start.2 = (s32[1,4,1024]{2,1,0:T(4,128)S(1)}, s32[1,4,1024]{2,1,0:T(4,128)}, u32[]{:S(2)}) copy-start(s32[1,4,1024]{2,1,0:T(4,128)} %param.15) | copy-start | bytes 49156
  138.0 10.5 %collective-permute-start = (bf16[1024,256]{1,0:T(8,128)(2,1)}, bf16[1024,256]{1,0:T(8,128)(2,1)}, u32[]{:S(2)}, u32[]{:S(2)}) collective-permute-start(bf16[1024,256]{1,0:T(8,128)(2,1)} %get-tuple-element.86), channel_id=1, source_target_pairs={{112,0},{0,16},{16,32},{32,48},{48,64},{64,80},{80,96},{96,112},{1... | collective-permute-start | bytes 1572872 | tf_op jit(solution)/shard_map/ppermute | solution.py:12
  141.0 9.4 %collective-permute-start.1 = (bf16[1024,256]{1,0:T(8,128)(2,1)}, bf16[1024,256]{1,0:T(8,128)(2,1)}, u32[]{:S(2)}, u32[]{:S(2)}) collective-permute-start(bf16[1024,256]{1,0:T(8,128)(2,1)} %get-tuple-element.85), channel_id=1, source_target_pairs={{16,0},{32,16},{48,32},{64,48},{80,64},{96,80},{112,96},{0,112},{1... | collective-permute-start | bytes 1572872 | tf_op jit(solution)/shard_map/ppermute | solution.py:12
  141.0 15.3 %collective-permute-start.2 = (bf16[1024,256]{1,0:T(8,128)(2,1)}, bf16[1024,256]{1,0:T(8,128)(2,1)S(1)}, u32[]{:S(2)}, u32[]{:S(2)}) collective-permute-start(bf16[1024,256]{1,0:T(8,128)(2,1)} %get-tuple-element.84), channel_id=1, source_target_pairs={{15,0},{0,1},{1,2},{2,3},{3,4},{4,5},{5,6},{6,7},{7,8},{8,9},{9,10... | collective-permute-start | bytes 1572872 | tf_op jit(solution)/shard_map/ppermute | solution.py:12
  142.3 5.4 %copy-start = (s32[6,4096]{1,0:T(8,128)S(1)}, s32[6,4096]{1,0:T(8,128)}, u32[]{:S(2)}) copy-start(s32[6,4096]{1,0:T(8,128)} %param.16) | copy-start | bytes 294916
  142.3 5.6 %copy-start.1 = (f32[6,4096]{1,0:T(8,128)S(1)}, f32[6,4096]{1,0:T(8,128)}, u32[]{:S(2)}) copy-start(f32[6,4096]{1,0:T(8,128)} %param.17) | copy-start | bytes 294916
  142.3 5.7 %copy-start.3 = (s32[128,16]{0,1:T(8,128)S(1)}, s32[128,16]{0,1:T(8,128)}, u32[]{:S(2)}) copy-start(s32[128,16]{0,1:T(8,128)} %param.18) | copy-start | bytes 24580
  142.3 5.9 %copy-start.4 = (s32[1,128]{1,0:T(1,128)S(1)}, s32[1,128]{1,0:T(1,128)}, u32[]{:S(2)}) copy-start(s32[1,128]{1,0:T(1,128)} %param.19) | copy-start | bytes 1540
  142.3 14.8 %collective-permute-start.3 = (bf16[1024,256]{1,0:T(8,128)(2,1)}, bf16[1024,256]{1,0:T(8,128)(2,1)S(1)}, u32[]{:S(2)}, u32[]{:S(2)}) collective-permute-start(bf16[1024,256]{1,0:T(8,128)(2,1)} %get-tuple-element.83), channel_id=1, source_target_pairs={{1,0},{2,1},{3,2},{4,3},{5,4},{6,5},{7,6},{8,7},{9,8},{10,9},{11,1... | collective-permute-start | bytes 1572872 | tf_op jit(solution)/shard_map/ppermute | solution.py:12
where the time goes:
time: 324 us; the launch traced here: 322 us
  local copies, waits for them, and re-layouts  179 us (55%)
  matrix products  83.6 us (26%)
  blocking collectives  29.6 us (9%)
  other arithmetic  16 us (5%)
  starting transfers between devices  8.24 us (3%)
  waiting for transfers between devices  4.04 us (1%)
    gather x6, local copies, waits for them, and re-layouts, body(): neighbour = jnp.take(extended, faces[face], axis=0).astype(jnp.float32)  112 us
    dot_general x12, matrix products, run_block(): jnp.einsum('rskb,ksbc->rsc', spread, kernels, preferred_element_type=jnp....  83.6 us
    all_to_all x1, blocking collectives, body(): lax.all_to_all(leaving, ('dx', 'dy'), split_axis=0, concat_axis=0, tiled=...  29.6 us
    gather x1, local copies, waits for them, and re-layouts, body(): jnp.take(coag, export_rows.reshape(4 * export_count), axis=0)  17 us
    convert_element_type x10, local copies, waits for them, and re-layouts, run_block(): operand = grain_state.astype(jnp.bfloat16)  16.2 us
    convert_element_type x1, other arithmetic, body(): updated = flux_sum.astype(jnp.bfloat16)  12.3 us
    unnamed x18, local copies, waits for them, and re-layouts  9.24 us
    gather x1, local copies, waits for them, and re-layouts, body(): jnp.take(updated, mig_ids.reshape(domains * capacity), axis=0)  8.5 us
  transfers between devices with their start and end apart: 4, of which 1 were waited for; matrix products, arithmetic and copies ran while one was open for 2% of the time, Pallas kernels for 0%

commit v1 on v0

v1 whole, which is shorter than its diff:
```python
import functools
import jax
import jax.numpy as jnp
from jax import lax
from jax.experimental import pallas as pl
from jax.experimental.pallas import tpu as pltpu
from jax.sharding import PartitionSpec as P

SUBSTEPS = 6
MESH = pl.DeviceIdType.MESH
f32, bf16, i32, i16 = jnp.float32, jnp.bfloat16, jnp.int32, jnp.int16
LANES = 128
CHUNK = 1024


def column(row):
    return jnp.broadcast_to(row, (LANES, LANES)).T


def interleave(wide, first, block):
    n = block.shape[0]
    wide[pl.ds(2 * first, n, stride=2), :] = block[:, :LANES]
    wide[pl.ds(2 * first + 1, n, stride=2), :] = block[:, LANES:]


def merged(wide, first, n):
    left = wide[pl.ds(2 * first, n, stride=2), :]
    right = wide[pl.ds(2 * first + 1, n, stride=2), :]
    return jnp.concatenate([left, right], axis=1)


def coag_kernel(blocks, cls_ref, dust_ref, ker_ref, ids_ref, coag_ref, out_ref, wide, picked, cls_wide, *rest):
    ids, sem = rest[:4], rest[4]
    step = pl.program_id(0)
    rows = dust_ref.shape[0]
    copies = [
        pltpu.make_async_copy(ids_ref.at[pl.ds(k * CHUNK, CHUNK)], ids[k], sem.at[k]) for k in range(4)
    ]

    @pl.when(step == 0)
    def _():
        for copy in copies:
            copy.start()

    for k in range(rows // LANES):
        cls_wide[k * LANES:(k + 1) * LANES, :] = column(cls_ref[k:k + 1, :])
    group = cls_wide[...]
    pair = (group >> 1).astype(i16)
    odd = (group & 1) == 1
    masks = [pair == p for p in range(4)]
    block = dust_ref[...].astype(f32)
    state = [block[:, :LANES], block[:, LANES:]]
    for substep in range(SUBSTEPS):
        following = []
        for s in range(2):
            operand = state[s].astype(bf16)
            zero = jnp.zeros_like(operand)
            spread = jnp.concatenate([jnp.where(m, operand, zero) for m in masks], axis=1)
            weights = jnp.concatenate(
                [jnp.concatenate([ker_ref[2 * p, s], ker_ref[2 * p + 1, s]], axis=1) for p in range(4)], axis=0
            )
            both = jnp.dot(spread, weights, preferred_element_type=f32)
            product = jnp.where(odd, both[:, LANES:], both[:, :LANES])
            mean_square = jnp.mean(state[s] * state[s], axis=1, keepdims=True)
            following.append(state[s] + product * (mean_square / (1.0 + mean_square)))
        state = following
    rounded = jnp.concatenate(state, axis=1).astype(bf16)
    coag_ref[...] = rounded
    interleave(wide, step * rows, rounded.astype(f32))

    @pl.when(step == blocks - 1)
    def _():
        for copy in copies:
            copy.wait()

        def pick(i, carry):
            for v in range(4):
                at = i * 4 + v
                for k in range(4):
                    row = pl.multiple_of(ids[k][at], 2)
                    picked[pl.ds(pl.multiple_of(2 * (k * CHUNK) + 2 * at, 2), 2), :] = wide[pl.ds(row, 2), :]
            return carry

        lax.fori_loop(0, CHUNK // 4, pick, 0)

        def narrow(i, carry):
            first = pl.multiple_of(i * 256, 256)
            out_ref[pl.ds(first, 256), :] = merged(picked, first, 256).astype(bf16)
            return carry

        lax.fori_loop(0, 4 * CHUNK // 256, narrow, 0)


def coagulate(dust, classes, kernels, export_flat):
    rows = dust.shape[0]
    block = 1024
    blocks = rows // block
    return pl.pallas_call(
        functools.partial(coag_kernel, blocks),
        grid=(blocks,),
        in_specs=[
            pl.BlockSpec((block // LANES, LANES), lambda i: (i, 0)),
            pl.BlockSpec((block, 256), lambda i: (i, 0)),
            pl.BlockSpec(kernels.shape, lambda i: (0, 0, 0, 0)),
            pl.BlockSpec(memory_space=pl.ANY),
        ],
        out_specs=[
            pl.BlockSpec((block, 256), lambda i: (i, 0)),
            pl.BlockSpec((4 * CHUNK, 256), lambda i: (0, 0)),
        ],
        out_shape=[
            jax.ShapeDtypeStruct((rows, 256), bf16),
            jax.ShapeDtypeStruct((4 * CHUNK, 256), bf16),
        ],
        scratch_shapes=[
            pltpu.VMEM((2 * rows, LANES), f32),
            pltpu.VMEM((8 * CHUNK, LANES), f32),
            pltpu.VMEM((block, LANES), i32),
            *[pltpu.SMEM((CHUNK,), i32)] * 4,
            pltpu.SemaphoreType.DMA((4,)),
        ],
        compiler_params=pltpu.CompilerParams(vmem_limit_bytes=56 << 20),
        name="coagulate",
    )(classes.reshape(rows // LANES, LANES), dust, kernels, export_flat)


def exchange_kernel(n_dx, n_dy, out_ref, ghost_ref, send_sem, recv_sem):
    a, b = lax.axis_index("dx"), lax.axis_index("dy")
    peers = [
        (lax.rem(a + 1, n_dx), b),
        (lax.rem(a + n_dx - 1, n_dx), b),
        (a, lax.rem(b + 1, n_dy)),
        (a, lax.rem(b + n_dy - 1, n_dy)),
    ]
    barrier = pltpu.get_barrier_semaphore()
    for peer in peers:
        pl.semaphore_signal(barrier, inc=1, device_id=peer, device_id_type=MESH)
    pl.semaphore_wait(barrier, 4)
    copies = []
    for k in (2, 3, 0, 1):
        copy = pltpu.make_async_remote_copy(
            src_ref=out_ref.at[pl.ds(k * CHUNK, CHUNK)],
            dst_ref=ghost_ref.at[pl.ds(k * CHUNK, CHUNK)],
            send_sem=send_sem.at[k],
            recv_sem=recv_sem.at[k],
            device_id=peers[k],
            device_id_type=MESH,
        )
        copy.start()
        copies.append(copy)
    for copy in copies:
        copy.wait()


def exchange(outbound, n_dx, n_dy):
    return pl.pallas_call(
        functools.partial(exchange_kernel, n_dx, n_dy),
        in_specs=[pl.BlockSpec(memory_space=pl.ANY)],
        out_specs=pl.BlockSpec(memory_space=pl.ANY),
        out_shape=jax.ShapeDtypeStruct(outbound.shape, outbound.dtype),
        scratch_shapes=[pltpu.SemaphoreType.DMA((4,)), pltpu.SemaphoreType.DMA((4,))],
        compiler_params=pltpu.CompilerParams(collective_id=0, has_side_effects=True),
        name="exchange",
    )(outbound)


FACES = 6
SPLIT = 4
UNROLL = 4


def diffuse_kernel(coag_ref, ghost_ref, coef_ref, faces_ref, mig_ref, count_ref, next_ref, leave_ref,
                   ext, coefs, wide, picked, *rest):
    ids, migs, sem = rest[:SPLIT * FACES], rest[SPLIT * FACES:SPLIT * FACES + 2], rest[-1]
    rows = coag_ref.shape[0]
    copies = []
    for f in range(FACES):
        for u in range(SPLIT):
            k = f * SPLIT + u
            copies.append(pltpu.make_async_copy(
                faces_ref.at[pl.ds(f * rows + u * CHUNK, CHUNK)], ids[k], sem.at[k]))
    for m in range(2):
        copies.append(pltpu.make_async_copy(
            mig_ref.at[pl.ds(m * CHUNK, CHUNK)], migs[m], sem.at[SPLIT * FACES + m]))
    for copy in copies:
        copy.start()

    def widen(i, carry):
        first = pl.multiple_of(i * 128, 128)
        interleave(ext, first, coag_ref[pl.ds(first, 128), :].astype(f32))
        interleave(ext, rows + first, ghost_ref[pl.ds(first, 128), :].astype(f32))
        return carry

    lax.fori_loop(0, rows // 128, widen, 0)

    def spread(i, carry):
        first = pl.multiple_of(i * LANES, LANES)
        block = coef_ref[:, pl.ds(first, LANES)]
        for f in range(FACES):
            coefs[pl.ds(pl.multiple_of(f * rows + first, LANES), LANES), :] = column(block[f:f + 1, :])
        kept = 1.0 - jnp.sum(block, axis=0, keepdims=True)
        coefs[pl.ds(pl.multiple_of(FACES * rows + first, LANES), LANES), :] = column(kept)
        return carry

    lax.fori_loop(0, rows // LANES, spread, 0)
    for copy in copies:
        copy.wait()

    def step(i, carry):
        for v in range(UNROLL):
            at = i * UNROLL + v
            for u in range(SPLIT):
                cell = u * CHUNK + at
                total = ext[pl.ds(pl.multiple_of(2 * cell, 2), 2), :] * coefs[
                    pl.ds(FACES * rows + cell, 2, stride=0), :]
                for f in range(FACES):
                    row = pl.multiple_of(ids[f * SPLIT + u][at], 2)
                    total = total + ext[pl.ds(row, 2), :] * coefs[pl.ds(f * rows + cell, 2, stride=0), :]
                wide[pl.ds(pl.multiple_of(2 * cell, 2), 2), :] = total
        return carry

    lax.fori_loop(0, CHUNK // UNROLL, step, 0)

    def narrow(i, carry):
        first = pl.multiple_of(i * 256, 256)
        next_ref[pl.ds(first, 256), :] = merged(wide, first, 256).astype(bf16)
        return carry

    lax.fori_loop(0, rows // 256, narrow, 0)

    def pick(i, carry):
        for v in range(8):
            at = i * 8 + v
            for m in range(2):
                row = pl.multiple_of(migs[m][at], 2)
                picked[pl.ds(pl.multiple_of(2 * (m * CHUNK) + 2 * at, 2), 2), :] = wide[pl.ds(row, 2), :]
        return carry

    lax.fori_loop(0, CHUNK // 8, pick, 0)
    slot = lax.broadcasted_iota(i32, (16, 256), 0)

    def leave(i, carry):
        for v in range(8):
            domain = i * 8 + v
            first = pl.multiple_of(domain * 16, 16)
            block = merged(picked, first, 16)
            leave_ref[pl.ds(first, 16), :] = jnp.where(slot < count_ref[domain], block, 0.0).astype(bf16)
        return carry

    lax.fori_loop(0, leave_ref.shape[0] // 128, leave, 0)


def diffuse(coag, ghosts, face_coef, faces_flat, mig_flat, counts):
    rows = coag.shape[0]
    vmem = pl.BlockSpec(memory_space=pltpu.VMEM)
    hbm = pl.BlockSpec(memory_space=pl.ANY)
    return pl.pallas_call(
        diffuse_kernel,
        in_specs=[vmem, vmem, vmem, hbm, hbm, pl.BlockSpec(memory_space=pltpu.SMEM)],
        out_specs=[vmem, vmem],
        out_shape=[
            jax.ShapeDtypeStruct((rows, 256), bf16),
            jax.ShapeDtypeStruct((2 * CHUNK, 256), bf16),
        ],
        scratch_shapes=[
            pltpu.VMEM((4 * rows, LANES), f32),
            pltpu.VMEM(((FACES + 1) * rows, LANES), f32),
            pltpu.VMEM((2 * rows, LANES), f32),
            pltpu.VMEM((4 * CHUNK, LANES), f32),
            *[pltpu.SMEM((CHUNK,), i32)] * (SPLIT * FACES + 2),
            pltpu.SemaphoreType.DMA((SPLIT * FACES + 2,)),
        ],
        compiler_params=pltpu.CompilerParams(vmem_limit_bytes=56 << 20),
        name="diffuse",
    )(coag, ghosts, face_coef, faces_flat, mig_flat, counts)


def migrate_kernel(n_dx, n_dy, leave_ref, arrive_ref, send_sem, recv_sem, own_sem):
    a, b = lax.axis_index("dx"), lax.axis_index("dy")
    me = a * n_dy + b
    count = n_dx * n_dy
    cap = leave_ref.shape[0] // count

    def greet(k, carry):
        peer = lax.rem(me + k, count)
        pl.semaphore_signal(
            pltpu.get_barrier_semaphore(), inc=1, device_id=(peer // n_dy, lax.rem(peer, n_dy)), device_id_type=MESH)
        return carry

    lax.fori_loop(1, count, greet, 0)
    pl.semaphore_wait(pltpu.get_barrier_semaphore(), count - 1)

    def block(peer):
        return pl.ds(pl.multiple_of(peer * cap, cap), cap)

    def remote(k):
        peer = lax.rem(me + k, count)
        return pltpu.make_async_remote_copy(
            src_ref=leave_ref.at[block(peer)],
            dst_ref=arrive_ref.at[block(me)],
            send_sem=send_sem.at[k],
            recv_sem=recv_sem.at[k],
            device_id=(peer // n_dy, lax.rem(peer, n_dy)),
            device_id_type=MESH,
        )

    own = pltpu.make_async_copy(leave_ref.at[block(me)], arrive_ref.at[block(me)], own_sem)
    own.start()

    def send(k, carry):
        remote(k).start()
        return carry

    lax.fori_loop(1, count, send, 0)
    own.wait()

    def finish(k, carry):
        remote(k).wait()
        return carry

    lax.fori_loop(1, count, finish, 0)


def migrate(leaving, n_dx, n_dy):
    count = n_dx * n_dy
    return pl.pallas_call(
        functools.partial(migrate_kernel, n_dx, n_dy),
        in_specs=[pl.BlockSpec(memory_space=pl.ANY)],
        out_specs=pl.BlockSpec(memory_space=pl.ANY),
        out_shape=jax.ShapeDtypeStruct(leaving.shape, leaving.dtype),
        scratch_shapes=[
            pltpu.SemaphoreType.DMA((count,)), pltpu.SemaphoreType.DMA((count,)), pltpu.SemaphoreType.DMA],
        compiler_params=pltpu.CompilerParams(collective_id=1, has_side_effects=True),
        name="migrate",
    )(leaving)


def body(n_dx, n_dy, dust, classes, kernels, export_ids, faces, face_coef, mig_ids, mig_counts):
    coag, outbound = coagulate(dust, classes, kernels, (export_ids * 2).reshape(-1))
    ghosts = exchange(outbound, n_dx, n_dy)
    updated, leaving = diffuse(
        coag, ghosts, face_coef, (faces * 2).reshape(-1), (mig_ids * 2).reshape(-1), mig_counts.reshape(-1))
    return updated, migrate(leaving, n_dx, n_dy)


def solution(mesh):
    return jax.shard_map(
        functools.partial(body, mesh.shape["dx"], mesh.shape["dy"]),
        mesh=mesh,
        in_specs=(
            P(("dx", "dy"), None),
            P(("dx", "dy")),
            P(),
            P(("dx", "dy"), None, None),
            P(None, ("dx", "dy")),
            P(None, ("dx", "dy")),
            P(("dx", "dy"), None),
            P(("dx", "dy"), None),
        ),
        out_specs=(P(("dx", "dy"), None), P(("dx", "dy"), None)),
        check_vma=False,
    )
```

time: 324 us -> 113 us (0.35)
  local copies, waits for them, and re-layouts: 179 us -> 4.33 us
  Pallas kernels: 0 us -> 105 us
  matrix products: 83.6 us -> 0 us
  blocking collectives: 29.6 us -> 0 us
  other arithmetic: 16 us -> 2.34 us
  starting transfers between devices: 8.24 us -> 0 us
  waiting for transfers between devices: 4.04 us -> 0 us
    gather x8 -> x0, local copies, waits for them, and re-layouts: 138 us -> none  [the longest x6 112 us: body(): neighbour = jnp.take(extended, faces[face], axis=0).astype(jnp.float32)]
    pallas_call x0 -> x4, Pallas kernels: none -> 105 us  [the longest x1 36.4 us: diffuse(): pl.pallas_call(diffuse_kernel, in_specs=[vmem, vmem, vmem, hbm, hbm, pl.B...]
    dot_general x12 -> x0, matrix products: 83.6 us -> none  [run_block(): jnp.einsum('rskb,ksbc->rsc', spread, kernels, preferred_element_type=jnp....]
    all_to_all x1 -> x0, blocking collectives: 29.6 us -> none  [body(): lax.all_to_all(leaving, ('dx', 'dy'), split_axis=0, concat_axis=0, tiled=...]
    convert_element_type x10 -> x0, local copies, waits for them, and re-layouts: 16.2 us -> none  [run_block(): operand = grain_state.astype(jnp.bfloat16)]
    convert_element_type x3 -> x0, other arithmetic: 12.3 us -> none  [the longest x1 12.3 us: body(): updated = flux_sum.astype(jnp.bfloat16)]
    ppermute x4 -> x0, starting transfers between devices: 8.24 us -> none  [passed_along(): return lax.ppermute(block, axis, route)]
    dynamic_slice x6 -> x0, local copies, waits for them, and re-layouts: 7.52 us -> none  [coagulate(): lax.map(run_block, (dust_rows.reshape(block_count, block_rows, species *...]
  transfers between devices with their start and end apart: 4 -> 0, of which waited for: 1 -> 0; matrix products, arithmetic and copies ran while one was open for 2% -> 0% of each run, Pallas kernels for 0% -> 0%
where the time goes in v1:
time: 113 us
  Pallas kernels  105 us (93%)
  local copies, waits for them, and re-layouts  4.33 us (4%)
  other arithmetic  2.34 us (2%)
    pallas_call x1, Pallas kernels, diffuse(): pl.pallas_call(diffuse_kernel, in_specs=[vmem, vmem, vmem, hbm, hbm, pl.B...  36.4 us
    pallas_call x1, Pallas kernels, migrate(): pl.pallas_call(functools.partial(migrate_kernel, n_dx, n_dy), in_specs=[p...  27.9 us
    pallas_call x1, Pallas kernels, coagulate(): pl.pallas_call(functools.partial(coag_kernel, blocks), grid=(blocks,), in...  22.3 us
    pallas_call x1, Pallas kernels, exchange(): pl.pallas_call(functools.partial(exchange_kernel, n_dx, n_dy), in_specs=[...  18.7 us
    unnamed x2, local copies, waits for them, and re-layouts  2.87 us

profile of v1, /device:TPU:1, one launch (start us, length us, event | category | flops | bytes accessed | tf_op | source)
XLA Modules:
  0.0 112.7 jit_solution(6923845758562029998)
XLA Ops:
  0.6 0.7 broadcast_multiply_fusion.1
  1.3 0.7 multiply_bitcast_fusion
  2.1 0.6 copy.13
  2.7 0.1 copy.10
  2.8 0.7 reshape.22.mig_ref
  3.4 0.9 broadcast_multiply_fusion
  4.4 0.7 reshape.21.faces_ref
  5.0 22.3 %coagulate.1 = (bf16[4096,256]{1,0:T(8,128)(2,1)}, bf16[4096,256]{1,0:T(8,128)(2,1)}) custom-call(s32[32,128]{1,0:T(8,128)} %bitcast.8, bf16[4096,256]{1,0:T(8,128)(2,1)} %dust_ref.1, bf16[8,2,128,128]{3,2,1,0:T(8,128)(2,1)} %ker_ref.1, s32[4096]{0:T(1024)} %bitcast.7), custom_call_target="tpu_custom_call" | custom-call | tf_op jit(solution)/shard_map/coagulate/pallas_call | solution.py:98
  27.3 18.7 %exchange.1.ghost_ref = bf16[4096,256]{1,0:T(8,128)(2,1)} custom-call(bf16[4096,256]{1,0:T(8,128)(2,1)} %get-tuple-element.7.out_ref), custom_call_target="tpu_custom_call" | custom-call | tf_op jit(solution)/shard_map/exchange/pallas_call | solution.py:156
  46.0 36.4 %diffuse.1 = (bf16[4096,256]{1,0:T(8,128)(2,1)}, bf16[2048,256]{1,0:T(8,128)(2,1)}) custom-call(bf16[4096,256]{1,0:T(8,128)(2,1)} %get-tuple-element.6.coag_ref, bf16[4096,256]{1,0:T(8,128)(2,1)} %exchange.1.ghost_ref, f32[6,4096]{1,0:T(8,128)} %coef_ref.1, s32[24576]{0:T(1024)} %reshape.21.faces_ref, s32[2048]{0:T(1024)} %reshape.22.mig_ref, s32[128]{0:T(128)} %bitcast.9), custom_call_target="tpu_custom_call" | custom-call | tf_op jit(solution)/shard_map/diffuse/pallas_call | solution.py:257
  82.5 27.9 %migrate.1 = bf16[2048,256]{1,0:T(8,128)(2,1)} custom-call(bf16[2048,256]{1,0:T(8,128)(2,1)} %get-tuple-element.9.leave_ref), custom_call_target="tpu_custom_call" | custom-call | tf_op jit(solution)/shard_map/migrate/pallas_call | solution.py:326
  110.4 2.3 %copy.15 = bf16[2048,256]{1,0:T(8,128)(2,1)} copy(bf16[2048,256]{1,0:T(8,128)(2,1)} %migrate.1) | data formatting | bytes 2097152

commit v2 on v1

v2 whole, which is shorter than its diff:
```python
import functools
import jax
import jax.numpy as jnp
from jax import lax
from jax.experimental import pallas as pl
from jax.experimental.pallas import tpu as pltpu
from jax.sharding import PartitionSpec as P

SUBSTEPS = 6
MESH = pl.DeviceIdType.MESH
f32, bf16, i32, i16 = jnp.float32, jnp.bfloat16, jnp.int32, jnp.int16
LANES = 128
CHUNK = 1024


def column(row):
    return jnp.broadcast_to(row, (LANES, LANES)).T


def interleave(wide, first, block):
    n = block.shape[0]
    wide[pl.ds(2 * first, n, stride=2), :] = block[:, :LANES]
    wide[pl.ds(2 * first + 1, n, stride=2), :] = block[:, LANES:]


def merged(wide, first, n):
    left = wide[pl.ds(2 * first, n, stride=2), :]
    right = wide[pl.ds(2 * first + 1, n, stride=2), :]
    return jnp.concatenate([left, right], axis=1)


def coag_kernel(blocks, cls_ref, dust_ref, ker_ref, ids_ref, coag_ref, out_ref, wide, picked, cls_wide, scaled, *rest):
    ids, sem = rest[:4], rest[4]
    step = pl.program_id(0)
    rows = dust_ref.shape[0]
    copies = [pltpu.make_async_copy(scaled.at[pl.ds(k, 1), :], ids[k], sem.at[k]) for k in range(4)]

    @pl.when(step == 0)
    def _():
        scaled[...] = ids_ref[...] * 2
        for copy in copies:
            copy.start()

    for k in range(rows // LANES):
        cls_wide[k * LANES:(k + 1) * LANES, :] = column(cls_ref[k:k + 1, :])
    group = cls_wide[...]
    pair = (group >> 1).astype(i16)
    odd = (group & 1) == 1
    masks = [pair == p for p in range(4)]
    block = dust_ref[...].astype(f32)
    state = [block[:, :LANES], block[:, LANES:]]
    for substep in range(SUBSTEPS):
        following = []
        for s in range(2):
            operand = state[s].astype(bf16)
            zero = jnp.zeros_like(operand)
            spread = jnp.concatenate([jnp.where(m, operand, zero) for m in masks], axis=1)
            weights = jnp.concatenate(
                [jnp.concatenate([ker_ref[2 * p, s], ker_ref[2 * p + 1, s]], axis=1) for p in range(4)], axis=0
            )
            both = jnp.dot(spread, weights, preferred_element_type=f32)
            product = jnp.where(odd, both[:, LANES:], both[:, :LANES])
            mean_square = jnp.mean(state[s] * state[s], axis=1, keepdims=True)
            following.append(state[s] + product * (mean_square / (1.0 + mean_square)))
        state = following
    rounded = jnp.concatenate(state, axis=1).astype(bf16)
    coag_ref[...] = rounded
    interleave(wide, step * rows, rounded.astype(f32))

    @pl.when(step == blocks - 1)
    def _():
        for copy in copies:
            copy.wait()

        def pick(i, carry):
            for v in range(8):
                at = i * 8 + v
                for k in range(4):
                    row = pl.multiple_of(ids[k][0, at], 2)
                    picked[pl.ds(pl.multiple_of(2 * (k * CHUNK) + 2 * at, 2), 2), :] = wide[pl.ds(row, 2), :]
            return carry

        lax.fori_loop(0, CHUNK // 8, pick, 0)

        def narrow(i, carry):
            first = pl.multiple_of(i * 256, 256)
            out_ref[pl.ds(first, 256), :] = merged(picked, first, 256).astype(bf16)
            return carry

        lax.fori_loop(0, 4 * CHUNK // 256, narrow, 0)


def coagulate(dust, classes, kernels, export_ids):
    rows = dust.shape[0]
    block = 1024
    blocks = rows // block
    return pl.pallas_call(
        functools.partial(coag_kernel, blocks),
        grid=(blocks,),
        in_specs=[
            pl.BlockSpec((block // LANES, LANES), lambda i: (i, 0)),
            pl.BlockSpec((block, 256), lambda i: (i, 0)),
            pl.BlockSpec(kernels.shape, lambda i: (0, 0, 0, 0)),
            pl.BlockSpec(export_ids.shape, lambda i: (0, 0)),
        ],
        out_specs=[
            pl.BlockSpec((block, 256), lambda i: (i, 0)),
            pl.BlockSpec((4 * CHUNK, 256), lambda i: (0, 0)),
        ],
        out_shape=[
            jax.ShapeDtypeStruct((rows, 256), bf16),
            jax.ShapeDtypeStruct((4 * CHUNK, 256), bf16),
        ],
        scratch_shapes=[
            pltpu.VMEM((2 * rows, LANES), f32),
            pltpu.VMEM((8 * CHUNK, LANES), f32),
            pltpu.VMEM((block, LANES), i32),
            pltpu.VMEM(export_ids.shape, i32),
            *[pltpu.SMEM((1, CHUNK), i32)] * 4,
            pltpu.SemaphoreType.DMA((4,)),
        ],
        compiler_params=pltpu.CompilerParams(vmem_limit_bytes=56 << 20),
        name="coagulate",
    )(classes.reshape(rows // LANES, LANES), dust, kernels, export_ids)


FACES = 6
CAP = 16
UNROLL = 32


def step_kernel(n_dx, n_dy, outbound_ref, coag_ref, coef_ref, faces_ref, mig_ref, count_ref, next_ref, arrive_ref,
                ext, coefs, wide, picked, ghosts, leave, updated, scaled, *rest):
    ids = rest[:FACES]
    send_sem, recv_sem, ids_sem, own_sem, out_sem, leave_sem, arrive_sem = rest[FACES:]
    rows = coag_ref.shape[0]
    count = n_dx * n_dy
    a, b = lax.axis_index("dx"), lax.axis_index("dy")
    me = a * n_dy + b

    def position(device):
        return (device // n_dy, lax.rem(device, n_dy))

    def greet(k, carry):
        pl.semaphore_signal(
            pltpu.get_barrier_semaphore(), inc=1, device_id=position(lax.rem(me + k, count)), device_id_type=MESH)
        return carry

    lax.fori_loop(1, count, greet, 0)
    scaled[...] = faces_ref[...] * 2
    lookups = [pltpu.make_async_copy(scaled.at[pl.ds(f, 1), :], ids[f], ids_sem.at[f]) for f in range(FACES)]
    for copy in lookups:
        copy.start()
    pl.semaphore_wait(pltpu.get_barrier_semaphore(), count - 1)

    peers = [
        (lax.rem(a + 1, n_dx), b),
        (lax.rem(a + n_dx - 1, n_dx), b),
        (a, lax.rem(b + 1, n_dy)),
        (a, lax.rem(b + n_dy - 1, n_dy)),
    ]
    halo = {}
    for k in (2, 3, 0, 1):
        halo[k] = pltpu.make_async_remote_copy(
            src_ref=outbound_ref.at[pl.ds(k * CHUNK, CHUNK)],
            dst_ref=ghosts.at[pl.ds(k * CHUNK, CHUNK)],
            send_sem=send_sem.at[k],
            recv_sem=recv_sem.at[k],
            device_id=peers[k],
            device_id_type=MESH,
        )
        halo[k].start()

    def spread(i, carry):
        first = pl.multiple_of(i * LANES, LANES)
        block = coef_ref[:, pl.ds(first, LANES)]
        kept = 1.0 - jnp.sum(block, axis=0, keepdims=True)
        for f in range(FACES + 1):
            coefs[pl.ds(f * rows + first, LANES), :] = column(block[f:f + 1, :] if f < FACES else kept)
        interleave(ext, first, coag_ref[pl.ds(first, LANES), :].astype(f32))
        return carry

    lax.fori_loop(0, rows // LANES, spread, 0)
    for copy in lookups:
        copy.wait()
    for k in (0, 1, 2, 3):
        halo[k].wait()

        def widen(i, carry):
            first = pl.multiple_of(i * LANES, LANES)
            interleave(ext, rows + k * CHUNK + first, ghosts[pl.ds(k * CHUNK + first, LANES), :].astype(f32))
            return carry

        lax.fori_loop(0, CHUNK // LANES, widen, 0)

    def weighted(row, cell, f):
        return ext[pl.ds(row, 2), :] * coefs[pl.ds(f * rows + cell, 2, stride=0), :]

    def stay(i, carry):
        first = pl.multiple_of(i * UNROLL, UNROLL)
        for j in range(UNROLL):
            cell = first + j
            total = weighted(2 * cell, cell, FACES)
            for f in range(FACES):
                total = total + weighted(ids[f][0, cell], cell, f)
            wide[pl.ds(pl.multiple_of(2 * cell, 2), 2), :] = total
        updated[pl.ds(first, UNROLL), :] = merged(wide, first, UNROLL).astype(bf16)
        return carry

    lax.fori_loop(0, rows // UNROLL, stay, 0)
    out = pltpu.make_async_copy(updated, next_ref, out_sem)
    out.start()

    def place(domain):
        return pl.ds(pl.multiple_of(domain * CAP, CAP), CAP)

    slot = lax.broadcasted_iota(i32, (CAP, 256), 0)

    def pack(domain):
        for j in range(CAP):
            picked[pl.ds(2 * j, 2), :] = wide[pl.ds(2 * mig_ref[j, domain], 2), :]
        kept = jnp.clip(count_ref[0, domain] - slot, 0, 1).astype(f32)
        leave[place(domain), :] = (merged(picked, 0, CAP) * kept).astype(bf16)

    def send(k, carry):
        domain = lax.rem(me + k, count)
        pack(domain)
        pltpu.make_async_remote_copy(
            src_ref=leave.at[place(domain)],
            dst_ref=arrive_ref.at[place(me)],
            send_sem=leave_sem,
            recv_sem=arrive_sem,
            device_id=position(domain),
            device_id_type=MESH,
        ).start()
        return carry

    lax.fori_loop(1, count, send, 0)
    pack(me)
    own = pltpu.make_async_copy(leave.at[place(me)], arrive_ref.at[place(me)], own_sem)
    own.start()
    own.wait()
    others = pl.ds(0, (count - 1) * CAP)
    pltpu.make_async_copy(leave.at[others], leave.at[others], leave_sem).wait()
    pltpu.make_async_copy(arrive_ref.at[others], arrive_ref.at[others], arrive_sem).wait()
    out.wait()


def advance(outbound, coag, face_coef, faces, mig_ids, counts, n_dx, n_dy):
    rows = coag.shape[0]
    vmem = pl.BlockSpec(memory_space=pltpu.VMEM)
    smem = pl.BlockSpec(memory_space=pltpu.SMEM)
    hbm = pl.BlockSpec(memory_space=pl.ANY)
    moved = mig_ids.shape[0] * mig_ids.shape[1]
    dma = pltpu.SemaphoreType.DMA
    return pl.pallas_call(
        functools.partial(step_kernel, n_dx, n_dy),
        in_specs=[hbm, vmem, vmem, vmem, smem, smem],
        out_specs=[hbm, hbm],
        out_shape=[jax.ShapeDtypeStruct((rows, 256), bf16), jax.ShapeDtypeStruct((moved, 256), bf16)],
        scratch_shapes=[
            pltpu.VMEM((2 * rows + 2 * 4 * CHUNK, LANES), f32),
            pltpu.VMEM(((FACES + 1) * rows, LANES), f32),
            pltpu.VMEM((2 * rows, LANES), f32),
            pltpu.VMEM((2 * CAP, LANES), f32),
            pltpu.VMEM((4 * CHUNK, 256), bf16),
            pltpu.VMEM((moved, 256), bf16),
            pltpu.VMEM((rows, 256), bf16),
            pltpu.VMEM((FACES, rows), i32),
            *[pltpu.SMEM((1, rows), i32)] * FACES,
            dma((4,)), dma((4,)), dma((FACES,)), dma, dma, dma, dma,
        ],
        compiler_params=pltpu.CompilerParams(
            vmem_limit_bytes=56 << 20, collective_id=0, has_side_effects=True),
        name="advance",
    )(outbound, coag, face_coef, faces, mig_ids, counts)


def body(n_dx, n_dy, dust, classes, kernels, export_ids, faces, face_coef, mig_ids, mig_counts):
    coag, outbound = coagulate(dust, classes, kernels, export_ids[0])
    return advance(outbound, coag, face_coef, faces, mig_ids.T, mig_counts, n_dx, n_dy)


def solution(mesh):
    return jax.shard_map(
        functools.partial(body, mesh.shape["dx"], mesh.shape["dy"]),
        mesh=mesh,
        in_specs=(
            P(("dx", "dy"), None),
            P(("dx", "dy")),
            P(),
            P(("dx", "dy"), None, None),
            P(None, ("dx", "dy")),
            P(None, ("dx", "dy")),
            P(("dx", "dy"), None),
            P(("dx", "dy"), None),
        ),
        out_specs=(P(("dx", "dy"), None), P(("dx", "dy"), None)),
        check_vma=False,
    )
```

time: 113 us -> 92.3 us (0.82)
  Pallas kernels: 105 us -> 87.4 us
  other arithmetic: 2.34 us -> 0 us
    pallas_call x3 -> x1, Pallas kernels: 83.1 us -> 65.5 us  [advance(): pl.pallas_call(functools.partial(step_kernel, n_dx, n_dy), in_specs=[hbm,...]
    mul x2 -> x0, other arithmetic: 1.62 us -> none  [the longest x1 0.92 us: body(): faces * 2]
    reshape x2 -> x0, local copies, waits for them, and re-layouts: 1.36 us -> none  [the longest x1 0.68 us: body(): (faces * 2).reshape(-1)]
    unnamed x2 -> x4, local copies, waits for them, and re-layouts: 2.87 us -> 4.11 us
where the time goes in v2:
time: 92.3 us; the launch traced here: 92.2 us
  Pallas kernels  87.4 us (95%)
  local copies, waits for them, and re-layouts  4.11 us (4%)
    pallas_call x1, Pallas kernels, advance(): pl.pallas_call(functools.partial(step_kernel, n_dx, n_dy), in_specs=[hbm,...  65.5 us
    pallas_call x1, Pallas kernels, coagulate(): pl.pallas_call(functools.partial(coag_kernel, blocks), grid=(blocks,), in...  21.9 us
    unnamed x4, local copies, waits for them, and re-layouts  4.11 us

profile of v2, /device:TPU:1, one launch (start us, length us, event | category | flops | bytes accessed | tf_op | source)
XLA Modules:
  0.0 92.2 jit_solution(1166740403912978688)
XLA Ops:
  0.6 21.9 %coagulate.1 = (bf16[4096,256]{1,0:T(8,128)(2,1)}, bf16[4096,256]{1,0:T(8,128)(2,1)}) custom-call(s32[32,128]{1,0:T(8,128)} %bitcast.3, bf16[4096,256]{1,0:T(8,128)(2,1)} %dust_ref.1, bf16[8,2,128,128]{3,2,1,0:T(8,128)(2,1)} %ker_ref.1, s32[4,1024]{1,0:T(4,128)} %bitcast.4), custom_call_target="tpu_custom_call" | custom-call | tf_op jit(solution)/shard_map/coagulate/pallas_call | solution.py:97
  22.5 65.5 %advance.1 = (bf16[4096,256]{1,0:T(8,128)(2,1)}, bf16[2048,256]{1,0:T(8,128)(2,1)}) custom-call(bf16[4096,256]{1,0:T(8,128)(2,1)} %get-tuple-element.4.outbound_ref, bf16[4096,256]{1,0:T(8,128)(2,1)} %get-tuple-element.5.coag_ref, f32[6,4096]{1,0:T(8,128)} %coef_ref.1, s32[6,4096]{1,0:T(8,128)} %faces_ref.1, s32[16,128]{1,0:T(8,128)} %bitcast.5, ...), custom_call_target="tpu_custom_call" | custom-call | tf_op jit(solution)/shard_map/advance/pallas_call | solution.py:256
  88.0 0.0 copy-start
  88.1 3.1 %copy.12 = bf16[4096,256]{1,0:T(8,128)(2,1)} copy(bf16[4096,256]{1,0:T(8,128)(2,1)} %get-tuple-element.8) | data formatting | bytes 4194304
  91.2 0.0 copy-done
  91.2 1.0 %copy.13 = bf16[2048,256]{1,0:T(8,128)(2,1)} copy(bf16[2048,256]{1,0:T(8,128)(2,1)S(1)} %copy-done) | data formatting | bytes 2097152
Async XLA Ops:
  88.0 3.1 %copy-start = (bf16[2048,256]{1,0:T(8,128)(2,1)S(1)}, bf16[2048,256]{1,0:T(8,128)(2,1)}, u32[]{:S(2)}) copy-start(bf16[2048,256]{1,0:T(8,128)(2,1)} %get-tuple-element.9) | copy-start | bytes 3145732

commit v3 on v2

v3 whole, which is shorter than its diff:
```python
import functools
import jax
import jax.numpy as jnp
from jax import lax
from jax.experimental import pallas as pl
from jax.experimental.pallas import tpu as pltpu
from jax.sharding import PartitionSpec as P

SUBSTEPS = 6
SPECIES = 2
LANES = 128
FACES = 6
BLOCK = 1024
UNROLL = 32
MESH = pl.DeviceIdType.MESH
f32, bf16, i32, i16 = jnp.float32, jnp.bfloat16, jnp.int32, jnp.int16


def column(row):
    return jnp.broadcast_to(row, (LANES, LANES)).T


def merged(wide, first, n):
    return jnp.concatenate([wide[pl.ds(2 * first + s, n, stride=2), :] for s in range(SPECIES)], axis=1)


def step_kernel(n_dx, n_dy, dust_ref, cls_ref, ker_ref, export_ref, coef_ref, faces_ref, mig_ref, count_ref,
                next_ref, arrive_ref, ext, coefs, wide, picked, outbound, ghosts, leave, updated,
                scaled_faces, scaled_exports, cls_wide, *rest):
    ids, exports = rest[:FACES], rest[FACES:FACES + 4]
    send_sem, recv_sem, ids_sem, own_sem, out_sem, leave_sem, arrive_sem = rest[FACES + 4:]
    rows = dust_ref.shape[0]
    exported = export_ref.shape[1]
    cap = mig_ref.shape[0]
    count = n_dx * n_dy
    a, b = lax.axis_index("dx"), lax.axis_index("dy")
    me = a * n_dy + b

    def position(device):
        return (device // n_dy, lax.rem(device, n_dy))

    def greet(k, carry):
        pl.semaphore_signal(
            pltpu.get_barrier_semaphore(), inc=1, device_id=position(lax.rem(me + k, count)), device_id_type=MESH)
        return carry

    lax.fori_loop(1, count, greet, 0)

    scaled_exports[...] = export_ref[...] * 2
    scaled_faces[...] = faces_ref[...] * 2
    lookups = [
        pltpu.make_async_copy(scaled_exports.at[pl.ds(k, 1), :], exports[k], ids_sem.at[FACES + k]) for k in range(4)
    ] + [
        pltpu.make_async_copy(scaled_faces.at[pl.ds(f, 1), :], ids[f], ids_sem.at[f]) for f in range(FACES)
    ]
    for copy in lookups:
        copy.start()
    for k in range(rows // LANES):
        cls_wide[k * LANES:(k + 1) * LANES, :] = column(cls_ref[k:k + 1, :])

    def substeps(s):
        weights = [
            jnp.concatenate([ker_ref[2 * p, s], ker_ref[2 * p + 1, s]], axis=1) for p in range(ker_ref.shape[0] // 2)
        ]

        def run(i, carry):
            firsts = [pl.multiple_of((2 * i + h) * BLOCK, BLOCK) for h in range(2)]
            groups = [cls_wide[pl.ds(first, BLOCK), :] for first in firsts]
            odd = [(group & 1) == 1 for group in groups]
            pairs = [(group >> 1).astype(i16) for group in groups]
            state = [dust_ref[pl.ds(first, BLOCK), s * LANES:(s + 1) * LANES].astype(f32) for first in firsts]
            for substep in range(SUBSTEPS):
                for h in range(2):
                    operand = state[h].astype(bf16)
                    zero = jnp.zeros_like(operand)
                    spread = jnp.concatenate(
                        [jnp.where(pairs[h] == p, operand, zero) for p in range(len(weights))], axis=1)
                    both = jnp.dot(spread, jnp.concatenate(weights, axis=0), preferred_element_type=f32)
                    product = jnp.where(odd[h], both[:, LANES:], both[:, :LANES])
                    mean_square = jnp.mean(state[h] * state[h], axis=1, keepdims=True)
                    state[h] = state[h] + product * (mean_square / (1.0 + mean_square))
            for h in range(2):
                ext[pl.ds(2 * firsts[h] + s, BLOCK, stride=2), :] = state[h].astype(bf16).astype(f32)
            return carry

        lax.fori_loop(0, rows // (2 * BLOCK), run, 0)

    peers = [
        (lax.rem(a + 1, n_dx), b),
        (lax.rem(a + n_dx - 1, n_dx), b),
        (a, lax.rem(b + 1, n_dy)),
        (a, lax.rem(b + n_dy - 1, n_dy)),
    ]

    def halo(s, k):
        place = pl.ds(k * exported, exported)
        return pltpu.make_async_remote_copy(
            src_ref=outbound.at[s, place],
            dst_ref=ghosts.at[s, place],
            send_sem=send_sem.at[s * 4 + k],
            recv_sem=recv_sem.at[s * 4 + k],
            device_id=peers[k],
            device_id_type=MESH,
        )

    for s in range(SPECIES):
        substeps(s)
        if s == 0:
            for copy in lookups:
                copy.wait()
            pl.semaphore_wait(pltpu.get_barrier_semaphore(), count - 1)
        for k in (2, 3, 0, 1):

            def pick(i, carry):
                first = pl.multiple_of(i * UNROLL, UNROLL)
                for j in range(UNROLL):
                    picked[pl.ds(j, 1), :] = ext[pl.ds(exports[k][0, first + j] + s, 1), :]
                outbound[s, pl.ds(k * exported + first, UNROLL), :] = picked[...].astype(bf16)
                return carry

            lax.fori_loop(0, exported // UNROLL, pick, 0)
            halo(s, k).start()

    def spread(i, carry):
        first = pl.multiple_of(i * LANES, LANES)
        block = coef_ref[:, pl.ds(first, LANES)]
        kept = 1.0 - jnp.sum(block, axis=0, keepdims=True)
        for f in range(FACES + 1):
            coefs[pl.ds(f * rows + first, LANES), :] = column(block[f:f + 1, :] if f < FACES else kept)
        return carry

    lax.fori_loop(0, rows // LANES, spread, 0)
    for s in range(SPECIES):
        for k in (0, 1, 2, 3):
            halo(s, k).wait()

            def widen(i, carry):
                first = pl.multiple_of(i * LANES, LANES)
                at = rows + k * exported + first
                ext[pl.ds(2 * at + s, LANES, stride=2), :] = ghosts[
                    s, pl.ds(k * exported + first, LANES), :].astype(f32)
                return carry

            lax.fori_loop(0, exported // LANES, widen, 0)

    def weighted(row, cell, f):
        return ext[pl.ds(row, 2), :] * coefs[pl.ds(f * rows + cell, 2, stride=0), :]

    def stay(i, carry):
        first = pl.multiple_of(i * UNROLL, UNROLL)
        for j in range(UNROLL):
            cell = first + j
            total = weighted(2 * cell, cell, FACES)
            for f in range(FACES):
                total = total + weighted(ids[f][0, cell], cell, f)
            wide[pl.ds(2 * cell, 2), :] = total
        updated[pl.ds(first, UNROLL), :] = merged(wide, first, UNROLL).astype(bf16)
        return carry

    lax.fori_loop(0, rows // UNROLL, stay, 0)
    out = pltpu.make_async_copy(updated, next_ref, out_sem)
    out.start()

    def place(domain):
        return pl.ds(pl.multiple_of(domain * cap, cap), cap)

    slot = lax.broadcasted_iota(i32, (cap, SPECIES * LANES), 0)

    def pack(domain):
        for j in range(cap):
            picked[pl.ds(2 * j, 2), :] = wide[pl.ds(2 * mig_ref[j, domain], 2), :]
        kept = jnp.clip(count_ref[0, domain] - slot, 0, 1).astype(f32)
        leave[place(domain), :] = (merged(picked, 0, cap) * kept).astype(bf16)

    def send(k, carry):
        domain = lax.rem(me + k, count)
        pack(domain)
        pltpu.make_async_remote_copy(
            src_ref=leave.at[place(domain)],
            dst_ref=arrive_ref.at[place(me)],
            send_sem=leave_sem,
            recv_sem=arrive_sem,
            device_id=position(domain),
            device_id_type=MESH,
        ).start()
        return carry

    lax.fori_loop(1, count, send, 0)
    pack(me)
    own = pltpu.make_async_copy(leave.at[place(me)], arrive_ref.at[place(me)], own_sem)
    own.start()
    own.wait()
    others = pl.ds(0, (count - 1) * cap)
    pltpu.make_async_copy(leave.at[others], leave.at[others], leave_sem).wait()
    pltpu.make_async_copy(arrive_ref.at[others], arrive_ref.at[others], arrive_sem).wait()
    out.wait()


def advance(dust, classes, kernels, export_ids, face_coef, faces, mig_ids, counts, n_dx, n_dy):
    rows, width = dust.shape
    sent = export_ids.shape[0] * export_ids.shape[1]
    moved = mig_ids.shape[0] * mig_ids.shape[1]
    vmem = pl.BlockSpec(memory_space=pltpu.VMEM)
    smem = pl.BlockSpec(memory_space=pltpu.SMEM)
    hbm = pl.BlockSpec(memory_space=pl.ANY)
    dma = pltpu.SemaphoreType.DMA
    return pl.pallas_call(
        functools.partial(step_kernel, n_dx, n_dy),
        in_specs=[vmem] * 6 + [smem, smem],
        out_specs=[hbm, hbm],
        out_shape=[jax.ShapeDtypeStruct((rows, width), bf16), jax.ShapeDtypeStruct((moved, width), bf16)],
        scratch_shapes=[
            pltpu.VMEM((2 * (rows + sent), LANES), f32),
            pltpu.VMEM(((FACES + 1) * rows, LANES), f32),
            pltpu.VMEM((2 * rows, LANES), f32),
            pltpu.VMEM((UNROLL, LANES), f32),
            pltpu.VMEM((SPECIES, sent, LANES), bf16),
            pltpu.VMEM((SPECIES, sent, LANES), bf16),
            pltpu.VMEM((moved, width), bf16),
            pltpu.VMEM((rows, width), bf16),
            pltpu.VMEM(faces.shape, i32),
            pltpu.VMEM(export_ids.shape, i32),
            pltpu.VMEM((rows, LANES), i32),
            *[pltpu.SMEM((1, rows), i32)] * FACES,
            *[pltpu.SMEM((1, export_ids.shape[1]), i32)] * 4,
            dma((8,)), dma((8,)), dma((FACES + 4,)), dma, dma, dma, dma,
        ],
        compiler_params=pltpu.CompilerParams(
            vmem_limit_bytes=60 << 20, collective_id=0, has_side_effects=True),
        name="advance",
    )(dust, classes, kernels, export_ids, face_coef, faces, mig_ids, counts)


def hand_over_kernel(pieces, *refs):
    sources, targets, buffers, in_sem, out_sem = refs[:2], refs[2:4], refs[4:6], refs[6], refs[7]
    loads, stores = [], []
    for n in range(2):
        rows = sources[n].shape[0] // pieces
        for k in range(pieces):
            part = pl.ds(k * rows, rows)
            loads.append(pltpu.make_async_copy(sources[n].at[part], buffers[n].at[part], in_sem.at[n * pieces + k]))
            stores.append(pltpu.make_async_copy(buffers[n].at[part], targets[n].at[part], out_sem.at[n * pieces + k]))
    for load in loads:
        load.start()
    for load, store in zip(loads, stores):
        load.wait()
        store.start()
    for store in stores:
        store.wait()


def hand_over(*arrays):
    hbm = pl.BlockSpec(memory_space=pl.ANY)
    pieces = 4
    return pl.pallas_call(
        functools.partial(hand_over_kernel, pieces),
        in_specs=[hbm] * 2,
        out_specs=[hbm] * 2,
        out_shape=[jax.ShapeDtypeStruct(x.shape, x.dtype) for x in arrays],
        scratch_shapes=[
            *[pltpu.VMEM(x.shape, x.dtype) for x in arrays],
            pltpu.SemaphoreType.DMA((2 * pieces,)),
            pltpu.SemaphoreType.DMA((2 * pieces,)),
        ],
        name="hand_over",
    )(*arrays)


def body(n_dx, n_dy, dust, classes, kernels, export_ids, faces, face_coef, mig_ids, mig_counts):
    updated, arrivals = advance(
        dust, classes.reshape(-1, LANES), kernels, export_ids[0], face_coef, faces, mig_ids.T, mig_counts, n_dx, n_dy)
    return tuple(hand_over(updated, arrivals))


def solution(mesh):
    return jax.shard_map(
        functools.partial(body, mesh.shape["dx"], mesh.shape["dy"]),
        mesh=mesh,
        in_specs=(
            P(("dx", "dy"), None),
            P(("dx", "dy")),
            P(),
            P(("dx", "dy"), None, None),
            P(None, ("dx", "dy")),
            P(None, ("dx", "dy")),
            P(("dx", "dy"), None),
            P(("dx", "dy"), None),
        ),
        out_specs=(P(("dx", "dy"), None), P(("dx", "dy"), None)),
        check_vma=False,
    )
```

time: 92.3 us -> 82.9 us (0.90)
  Pallas kernels: 87.4 us -> 82.1 us
  local copies, waits for them, and re-layouts: 4.11 us -> 0 us
    pallas_call x2, Pallas kernels: 87.4 us -> 82.1 us  [the longest x1 79.3 us: advance(): pl.pallas_call(functools.partial(step_kernel, n_dx, n_dy), in_specs=[vmem...]
    unnamed x4 -> x0, local copies, waits for them, and re-layouts: 4.11 us -> none
where the time goes in v3:
time: 82.9 us; the launch traced here: 82.8 us
  Pallas kernels  82.1 us (99%)
    pallas_call x1, Pallas kernels, advance(): pl.pallas_call(functools.partial(step_kernel, n_dx, n_dy), in_specs=[vmem...  79.3 us
    pallas_call x1, Pallas kernels, hand_over(): pl.pallas_call(functools.partial(hand_over_kernel, pieces), in_specs=[hbm...  2.83 us

profile of v3, /device:TPU:1, one launch (start us, length us, event | category | flops | bytes accessed | tf_op | source)
XLA Modules:
  0.0 82.8 jit_solution(4478511476734019721)
XLA Ops:
  0.6 79.3 %advance.1 = (bf16[4096,256]{1,0:T(8,128)(2,1)}, bf16[2048,256]{1,0:T(8,128)(2,1)}) custom-call(bf16[4096,256]{1,0:T(8,128)(2,1)} %dust_ref.1, s32[32,128]{1,0:T(8,128)} %bitcast.3, bf16[8,2,128,128]{3,2,1,0:T(8,128)(2,1)} %ker_ref.1, s32[4,1024]{1,0:T(4,128)} %bitcast.4, f32[6,4096]{1,0:T(8,128)} %coef_ref.1, s32[6,4096]{1,0:T(8,128)} %faces_ref.1, ...), custom_call_target="tpu_custom_call" | custom-call | tf_op jit(solution)/shard_map/advance/pallas_call | solution.py:207
  79.9 2.8 %hand_over.1 = (bf16[4096,256]{1,0:T(8,128)(2,1)}, bf16[2048,256]{1,0:T(8,128)(2,1)}) custom-call(bf16[4096,256]{1,0:T(8,128)(2,1)} %get-tuple-element.4.refs_0_, bf16[2048,256]{1,0:T(8,128)(2,1)} %get-tuple-element.5.refs_1_), custom_call_target="tpu_custom_call" | custom-call | tf_op jit(solution)/shard_map/hand_over/pallas_call | solution.py:255

commit v4 on v3

--- a/solution.py
+++ b/solution.py
@@ -11,7 +11,10 @@
 LANES = 128
 FACES = 6
 BLOCK = 1024
-UNROLL = 32
+PARTS = 4
+UNROLL = 16
+PICKS = 8
+PICK_UNROLL = 4
 MESH = pl.DeviceIdType.MESH
 f32, bf16, i32, i16 = jnp.float32, jnp.bfloat16, jnp.int32, jnp.int16
 
@@ -25,34 +28,54 @@
 
 
 def step_kernel(n_dx, n_dy, dust_ref, cls_ref, ker_ref, export_ref, coef_ref, faces_ref, mig_ref, count_ref,
-                next_ref, arrive_ref, ext, coefs, wide, picked, outbound, ghosts, leave, updated,
+                next_ref, arrive_ref, dust, kernels, ext, coefs, wide, picked, outbound, ghosts, leave, updated,
                 scaled_faces, scaled_exports, cls_wide, *rest):
-    ids, exports = rest[:FACES], rest[FACES:FACES + 4]
-    send_sem, recv_sem, ids_sem, own_sem, out_sem, leave_sem, arrive_sem = rest[FACES + 4:]
+    ids, exports = rest[:FACES * PARTS], rest[FACES * PARTS:FACES * PARTS + 4 * PICKS]
+    load_sem, send_sem, recv_sem, ids_sem, own_sem, out_sem, leave_sem, arrive_sem = rest[FACES * PARTS + 4 * PICKS:]
     rows = dust_ref.shape[0]
     exported = export_ref.shape[1]
     cap = mig_ref.shape[0]
     count = n_dx * n_dy
+    part_rows, pick_rows = rows // PARTS, exported // PICKS
     a, b = lax.axis_index("dx"), lax.axis_index("dy")
     me = a * n_dy + b
 
     def position(device):
         return (device // n_dy, lax.rem(device, n_dy))
 
-    def greet(k, carry):
+    loads = [pltpu.make_async_copy(ker_ref, kernels, load_sem.at[0])]
+    for n in range(rows // (2 * BLOCK)):
+        part = pl.ds(n * 2 * BLOCK, 2 * BLOCK)
+        loads.append(pltpu.make_async_copy(dust_ref.at[part], dust.at[part], load_sem.at[1 + n]))
+    for copy in loads:
+        copy.start()
+
+    def greet(k):
         pl.semaphore_signal(
             pltpu.get_barrier_semaphore(), inc=1, device_id=position(lax.rem(me + k, count)), device_id_type=MESH)
+
+    def greet_eight(i, carry):
+        for j in range(8):
+            greet(8 * i + j)
         return carry
 
-    lax.fori_loop(1, count, greet, 0)
+    for k in range(1, 8):
+        greet(k)
+    lax.fori_loop(1, count // 8, greet_eight, 0)
 
     scaled_exports[...] = export_ref[...] * 2
     scaled_faces[...] = faces_ref[...] * 2
-    lookups = [
-        pltpu.make_async_copy(scaled_exports.at[pl.ds(k, 1), :], exports[k], ids_sem.at[FACES + k]) for k in range(4)
-    ] + [
-        pltpu.make_async_copy(scaled_faces.at[pl.ds(f, 1), :], ids[f], ids_sem.at[f]) for f in range(FACES)
-    ]
+    lookups = []
+    for k in range(4):
+        for u in range(PICKS):
+            n = k * PICKS + u
+            lookups.append(pltpu.make_async_copy(
+                scaled_exports.at[pl.ds(k, 1), pl.ds(u * pick_rows, pick_rows)], exports[n], ids_sem.at[n]))
+    for f in range(FACES):
+        for u in range(PARTS):
+            n = f * PARTS + u
+            lookups.append(pltpu.make_async_copy(
+                scaled_faces.at[pl.ds(f, 1), pl.ds(u * part_rows, part_rows)], ids[n], ids_sem.at[4 * PICKS + n]))
     for copy in lookups:
         copy.start()
     for k in range(rows // LANES):
@@ -60,7 +83,7 @@
 
     def substeps(s):
         weights = [
-            jnp.concatenate([ker_ref[2 * p, s], ker_ref[2 * p + 1, s]], axis=1) for p in range(ker_ref.shape[0] // 2)
+            jnp.concatenate([kernels[2 * p, s], kernels[2 * p + 1, s]], axis=1) for p in range(kernels.shape[0] // 2)
         ]
 
         def run(i, carry):
@@ -68,7 +91,7 @@
             groups = [cls_wide[pl.ds(first, BLOCK), :] for first in firsts]
             odd = [(group & 1) == 1 for group in groups]
             pairs = [(group >> 1).astype(i16) for group in groups]
-            state = [dust_ref[pl.ds(first, BLOCK), s * LANES:(s + 1) * LANES].astype(f32) for first in firsts]
+            state = [dust[pl.ds(first, BLOCK), s * LANES:(s + 1) * LANES].astype(f32) for first in firsts]
             for substep in range(SUBSTEPS):
                 for h in range(2):
                     operand = state[h].astype(bf16)
@@ -77,8 +100,8 @@
                         [jnp.where(pairs[h] == p, operand, zero) for p in range(len(weights))], axis=1)
                     both = jnp.dot(spread, jnp.concatenate(weights, axis=0), preferred_element_type=f32)
                     product = jnp.where(odd[h], both[:, LANES:], both[:, :LANES])
-                    mean_square = jnp.mean(state[h] * state[h], axis=1, keepdims=True)
-                    state[h] = state[h] + product * (mean_square / (1.0 + mean_square))
+                    squares = jnp.sum(state[h] * state[h], axis=1, keepdims=True)
+                    state[h] = state[h] + product * (squares / (LANES + squares))
             for h in range(2):
                 ext[pl.ds(2 * firsts[h] + s, BLOCK, stride=2), :] = state[h].astype(bf16).astype(f32)
             return carry
@@ -103,6 +126,8 @@
             device_id_type=MESH,
         )
 
+    for copy in loads:
+        copy.wait()
     for s in range(SPECIES):
         substeps(s)
         if s == 0:
@@ -112,21 +137,29 @@
         for k in (2, 3, 0, 1):
 
             def pick(i, carry):
-                first = pl.multiple_of(i * UNROLL, UNROLL)
-                for j in range(UNROLL):
-                    picked[pl.ds(j, 1), :] = ext[pl.ds(exports[k][0, first + j] + s, 1), :]
-                outbound[s, pl.ds(k * exported + first, UNROLL), :] = picked[...].astype(bf16)
+                for v in range(PICK_UNROLL):
+                    at = i * PICK_UNROLL + v
+                    for u in range(PICKS):
+                        row = exports[k * PICKS + u][0, at] + s
+                        picked[pl.ds(u * pick_rows + at, 1), :] = ext[pl.ds(row, 1), :]
                 return carry
 
-            lax.fori_loop(0, exported // UNROLL, pick, 0)
+            lax.fori_loop(0, pick_rows // PICK_UNROLL, pick, 0)
+
+            def narrow(i, carry):
+                first = pl.multiple_of(i * 256, 256)
+                outbound[s, pl.ds(k * exported + first, 256), :] = picked[pl.ds(first, 256), :].astype(bf16)
+                return carry
+
+            lax.fori_loop(0, exported // 256, narrow, 0)
             halo(s, k).start()
 
     def spread(i, carry):
         first = pl.multiple_of(i * LANES, LANES)
-        block = coef_ref[:, pl.ds(first, LANES)]
-        kept = 1.0 - jnp.sum(block, axis=0, keepdims=True)
-        for f in range(FACES + 1):
-            coefs[pl.ds(f * rows + first, LANES), :] = column(block[f:f + 1, :] if f < FACES else kept)
+        for f in range(FACES):
+            weight = column(coef_ref[f:f + 1, pl.ds(first, LANES)])
+            for half in range(2):
+                coefs[pl.ds(2 * (f * rows + first) + half, LANES, stride=2), :] = weight
         return carry
 
     lax.fori_loop(0, rows // LANES, spread, 0)
@@ -143,21 +176,22 @@
 
             lax.fori_loop(0, exported // LANES, widen, 0)
 
-    def weighted(row, cell, f):
-        return ext[pl.ds(row, 2), :] * coefs[pl.ds(f * rows + cell, 2, stride=0), :]
-
     def stay(i, carry):
-        first = pl.multiple_of(i * UNROLL, UNROLL)
-        for j in range(UNROLL):
-            cell = first + j
-            total = weighted(2 * cell, cell, FACES)
-            for f in range(FACES):
-                total = total + weighted(ids[f][0, cell], cell, f)
-            wide[pl.ds(2 * cell, 2), :] = total
-        updated[pl.ds(first, UNROLL), :] = merged(wide, first, UNROLL).astype(bf16)
+        at = pl.multiple_of(i * UNROLL, UNROLL)
+        for u in range(PARTS):
+            first = pl.multiple_of(u * part_rows + at, UNROLL)
+            for j in range(UNROLL):
+                pair = 2 * (first + j)
+                own = ext[pl.ds(pair, 2), :]
+                total = own
+                for f in range(FACES):
+                    row = ids[f * PARTS + u][0, at + j]
+                    total = total + coefs[pl.ds(2 * f * rows + pair, 2), :] * (ext[pl.ds(row, 2), :] - own)
+                wide[pl.ds(pair, 2), :] = total
+            updated[pl.ds(first, UNROLL), :] = merged(wide, first, UNROLL).astype(bf16)
         return carry
 
-    lax.fori_loop(0, rows // UNROLL, stay, 0)
+    lax.fori_loop(0, part_rows // UNROLL, stay, 0)
     out = pltpu.make_async_copy(updated, next_ref, out_sem)
     out.start()
 
@@ -206,14 +240,16 @@
     dma = pltpu.SemaphoreType.DMA
     return pl.pallas_call(
         functools.partial(step_kernel, n_dx, n_dy),
-        in_specs=[vmem] * 6 + [smem, smem],
+        in_specs=[hbm, vmem, hbm, vmem, vmem, vmem, smem, smem],
         out_specs=[hbm, hbm],
         out_shape=[jax.ShapeDtypeStruct((rows, width), bf16), jax.ShapeDtypeStruct((moved, width), bf16)],
         scratch_shapes=[
+            pltpu.VMEM(dust.shape, bf16),
+            pltpu.VMEM(kernels.shape, bf16),
             pltpu.VMEM((2 * (rows + sent), LANES), f32),
-            pltpu.VMEM(((FACES + 1) * rows, LANES), f32),
+            pltpu.VMEM((2 * FACES * rows, LANES), f32),
             pltpu.VMEM((2 * rows, LANES), f32),
-            pltpu.VMEM((UNROLL, LANES), f32),
+            pltpu.VMEM((export_ids.shape[1], LANES), f32),
             pltpu.VMEM((SPECIES, sent, LANES), bf16),
             pltpu.VMEM((SPECIES, sent, LANES), bf16),
             pltpu.VMEM((moved, width), bf16),
@@ -221,9 +257,10 @@
             pltpu.VMEM(faces.shape, i32),
             pltpu.VMEM(export_ids.shape, i32),
             pltpu.VMEM((rows, LANES), i32),
-            *[pltpu.SMEM((1, rows), i32)] * FACES,
-            *[pltpu.SMEM((1, export_ids.shape[1]), i32)] * 4,
-            dma((8,)), dma((8,)), dma((FACES + 4,)), dma, dma, dma, dma,
+            *[pltpu.SMEM((1, rows // PARTS), i32)] * (FACES * PARTS),
+            *[pltpu.SMEM((1, export_ids.shape[1] // PICKS), i32)] * (4 * PICKS),
+            dma((1 + rows // (2 * BLOCK),)), dma((8,)), dma((8,)), dma((FACES * PARTS + 4 * PICKS,)),
+            dma, dma, dma, dma,
         ],
         compiler_params=pltpu.CompilerParams(
             vmem_limit_bytes=60 << 20, collective_id=0, has_side_effects=True),

time: 82.9 us -> 78.3 us (0.945)
  Pallas kernels: 82.1 us -> 77.5 us
    pallas_call x1, Pallas kernels: 79.3 us -> 74.7 us  [advance(): pl.pallas_call(functools.partial(step_kernel, n_dx, n_dy), in_specs=[hbm,...]
where the time goes in v4:
time: 78.3 us; the launch traced here: 78.2 us
  Pallas kernels  77.5 us (99%)
    pallas_call x1, Pallas kernels, advance(): pl.pallas_call(functools.partial(step_kernel, n_dx, n_dy), in_specs=[hbm,...  74.7 us
    pallas_call x1, Pallas kernels, hand_over(): pl.pallas_call(functools.partial(hand_over_kernel, pieces), in_specs=[hbm...  2.83 us

profile of v4, /device:TPU:1, one launch (start us, length us, event | category | flops | bytes accessed | tf_op | source)
XLA Modules:
  0.0 78.2 jit_solution(15787371059457102273)
XLA Ops:
  0.6 74.7 %advance.1 = (bf16[4096,256]{1,0:T(8,128)(2,1)}, bf16[2048,256]{1,0:T(8,128)(2,1)}) custom-call(bf16[4096,256]{1,0:T(8,128)(2,1)} %dust_ref.1, s32[32,128]{1,0:T(8,128)} %bitcast.3, bf16[8,2,128,128]{3,2,1,0:T(8,128)(2,1)} %ker_ref.1, s32[4,1024]{1,0:T(4,128)} %bitcast.4, f32[6,4096]{1,0:T(8,128)} %coef_ref.1, s32[6,4096]{1,0:T(8,128)} %faces_ref.1, ...), custom_call_target="tpu_custom_call" | custom-call | tf_op jit(solution)/shard_map/advance/pallas_call | solution.py:241
  75.3 2.8 %hand_over.1 = (bf16[4096,256]{1,0:T(8,128)(2,1)}, bf16[2048,256]{1,0:T(8,128)(2,1)}) custom-call(bf16[4096,256]{1,0:T(8,128)(2,1)} %get-tuple-element.4.refs_0_, bf16[2048,256]{1,0:T(8,128)(2,1)} %get-tuple-element.5.refs_1_), custom_call_target="tpu_custom_call" | custom-call | tf_op jit(solution)/shard_map/hand_over/pallas_call | solution.py:292

commit v5 on v4

--- a/solution.py
+++ b/solution.py
@@ -11,8 +11,8 @@
 LANES = 128
 FACES = 6
 BLOCK = 1024
-PARTS = 4
-UNROLL = 16
+PARTS = 1
+UNROLL = 32
 PICKS = 8
 PICK_UNROLL = 4
 MESH = pl.DeviceIdType.MESH
@@ -50,18 +50,19 @@
     for copy in loads:
         copy.start()
 
-    def greet(k):
-        pl.semaphore_signal(
-            pltpu.get_barrier_semaphore(), inc=1, device_id=position(lax.rem(me + k, count)), device_id_type=MESH)
-
-    def greet_eight(i, carry):
-        for j in range(8):
-            greet(8 * i + j)
+    def greet(peer):
+        pl.semaphore_signal(pltpu.get_barrier_semaphore(), inc=1, device_id=peer, device_id_type=MESH)
+
+    for k in range(1, n_dy):
+        greet((a, lax.rem(b + k, n_dy)))
+
+    def greet_row(k, carry):
+        other = lax.rem(a + k, n_dx)
+        for peer in range(n_dy):
+            greet((other, peer))
         return carry
 
-    for k in range(1, 8):
-        greet(k)
-    lax.fori_loop(1, count // 8, greet_eight, 0)
+    lax.fori_loop(1, n_dx, greet_row, 0)
 
     scaled_exports[...] = export_ref[...] * 2
     scaled_faces[...] = faces_ref[...] * 2

time: 78.3 us -> 72.8 us (0.930)
  Pallas kernels: 77.5 us -> 72 us
    pallas_call x1, Pallas kernels: 74.7 us -> 69.1 us  [advance(): pl.pallas_call(functools.partial(step_kernel, n_dx, n_dy), in_specs=[hbm,...]
where the time goes in v5:
time: 72.8 us; the launch traced here: 72.6 us
  Pallas kernels  72 us (99%)
    pallas_call x1, Pallas kernels, advance(): pl.pallas_call(functools.partial(step_kernel, n_dx, n_dy), in_specs=[hbm,...  69.1 us
    pallas_call x1, Pallas kernels, hand_over(): pl.pallas_call(functools.partial(hand_over_kernel, pieces), in_specs=[hbm...  2.83 us

profile of v5, /device:TPU:1, one launch (start us, length us, event | category | flops | bytes accessed | tf_op | source)
XLA Modules:
  0.0 72.6 jit_solution(4907286046177606615)
XLA Ops:
  0.6 69.1 %advance.1 = (bf16[4096,256]{1,0:T(8,128)(2,1)}, bf16[2048,256]{1,0:T(8,128)(2,1)}) custom-call(bf16[4096,256]{1,0:T(8,128)(2,1)} %dust_ref.1, s32[32,128]{1,0:T(8,128)} %bitcast.3, bf16[8,2,128,128]{3,2,1,0:T(8,128)(2,1)} %ker_ref.1, s32[4,1024]{1,0:T(4,128)} %bitcast.4, f32[6,4096]{1,0:T(8,128)} %coef_ref.1, s32[6,4096]{1,0:T(8,128)} %faces_ref.1, ...), custom_call_target="tpu_custom_call" | custom-call | tf_op jit(solution)/shard_map/advance/pallas_call | solution.py:242
  69.8 2.8 %hand_over.1 = (bf16[4096,256]{1,0:T(8,128)(2,1)}, bf16[2048,256]{1,0:T(8,128)(2,1)}) custom-call(bf16[4096,256]{1,0:T(8,128)(2,1)} %get-tuple-element.4.refs_0_, bf16[2048,256]{1,0:T(8,128)(2,1)} %get-tuple-element.5.refs_1_), custom_call_target="tpu_custom_call" | custom-call | tf_op jit(solution)/shard_map/hand_over/pallas_call | solution.py:293

commit v6 on v5

--- a/solution.py
+++ b/solution.py
@@ -14,7 +14,7 @@
 PARTS = 1
 UNROLL = 32
 PICKS = 8
-PICK_UNROLL = 4
+PICK_UNROLL = 8
 MESH = pl.DeviceIdType.MESH
 f32, bf16, i32, i16 = jnp.float32, jnp.bfloat16, jnp.int32, jnp.int16
 
@@ -207,8 +207,7 @@
         kept = jnp.clip(count_ref[0, domain] - slot, 0, 1).astype(f32)
         leave[place(domain), :] = (merged(picked, 0, cap) * kept).astype(bf16)
 
-    def send(k, carry):
-        domain = lax.rem(me + k, count)
+    def ship(domain):
         pack(domain)
         pltpu.make_async_remote_copy(
             src_ref=leave.at[place(domain)],
@@ -218,9 +217,14 @@
             device_id=position(domain),
             device_id_type=MESH,
         ).start()
+
+    def send(k, carry):
+        ship(lax.rem(me + count // 2 - k, count))
+        ship(lax.rem(me + count // 2 + k, count))
         return carry
 
-    lax.fori_loop(1, count, send, 0)
+    ship(lax.rem(me + count // 2, count))
+    lax.fori_loop(1, count // 2, send, 0)
     pack(me)
     own = pltpu.make_async_copy(leave.at[place(me)], arrive_ref.at[place(me)], own_sem)
     own.start()

time: 72.8 us -> 71.6 us (0.984)
  Pallas kernels: 72 us -> 70.2 us
    pallas_call x1, Pallas kernels: 69.1 us -> 67.4 us  [advance(): pl.pallas_call(functools.partial(step_kernel, n_dx, n_dy), in_specs=[hbm,...]
where the time goes in v6:
time: 71.6 us; the launch traced here: 70.9 us
  Pallas kernels  70.2 us (98%)
    pallas_call x1, Pallas kernels, advance(): pl.pallas_call(functools.partial(step_kernel, n_dx, n_dy), in_specs=[hbm,...  67.4 us
    pallas_call x1, Pallas kernels, hand_over(): pl.pallas_call(functools.partial(hand_over_kernel, pieces), in_specs=[hbm...  2.83 us

profile of v6, /device:TPU:1, one launch (start us, length us, event | category | flops | bytes accessed | tf_op | source)
XLA Modules:
  0.0 70.9 jit_solution(5663112050056364052)
XLA Ops:
  0.6 67.4 %advance.1 = (bf16[4096,256]{1,0:T(8,128)(2,1)}, bf16[2048,256]{1,0:T(8,128)(2,1)}) custom-call(bf16[4096,256]{1,0:T(8,128)(2,1)} %dust_ref.1, s32[32,128]{1,0:T(8,128)} %bitcast.3, bf16[8,2,128,128]{3,2,1,0:T(8,128)(2,1)} %ker_ref.1, s32[4,1024]{1,0:T(4,128)} %bitcast.4, f32[6,4096]{1,0:T(8,128)} %coef_ref.1, s32[6,4096]{1,0:T(8,128)} %faces_ref.1, ...), custom_call_target="tpu_custom_call" | custom-call | tf_op jit(solution)/shard_map/advance/pallas_call | solution.py:246
  68.0 2.8 %hand_over.1 = (bf16[4096,256]{1,0:T(8,128)(2,1)}, bf16[2048,256]{1,0:T(8,128)(2,1)}) custom-call(bf16[4096,256]{1,0:T(8,128)(2,1)} %get-tuple-element.4.refs_0_, bf16[2048,256]{1,0:T(8,128)(2,1)} %get-tuple-element.5.refs_1_), custom_call_target="tpu_custom_call" | custom-call | tf_op jit(solution)/shard_map/hand_over/pallas_call | solution.py:297

commit v7 on v6

--- a/solution.py
+++ b/solution.py
@@ -12,7 +12,7 @@
 FACES = 6
 BLOCK = 1024
 PARTS = 1
-UNROLL = 32
+UNROLL = 64
 PICKS = 8
 PICK_UNROLL = 8
 MESH = pl.DeviceIdType.MESH

time: 71.6 us -> 71.2 us (level)
  Pallas kernels: 70.2 us -> 69.3 us
    pallas_call x1, Pallas kernels: 67.4 us -> 66.5 us  [advance(): pl.pallas_call(functools.partial(step_kernel, n_dx, n_dy), in_specs=[hbm,...]
where the time goes in v7:
time: 71.2 us; the launch traced here: 70 us
  Pallas kernels  69.3 us (97%)
    pallas_call x1, Pallas kernels, advance(): pl.pallas_call(functools.partial(step_kernel, n_dx, n_dy), in_specs=[hbm,...  66.5 us
    pallas_call x1, Pallas kernels, hand_over(): pl.pallas_call(functools.partial(hand_over_kernel, pieces), in_specs=[hbm...  2.83 us

profile of v7, /device:TPU:1, one launch (start us, length us, event | category | flops | bytes accessed | tf_op | source)
XLA Modules:
  0.0 70.0 jit_solution(5631200909489862130)
XLA Ops:
  0.6 66.5 %advance.1 = (bf16[4096,256]{1,0:T(8,128)(2,1)}, bf16[2048,256]{1,0:T(8,128)(2,1)}) custom-call(bf16[4096,256]{1,0:T(8,128)(2,1)} %dust_ref.1, s32[32,128]{1,0:T(8,128)} %bitcast.3, bf16[8,2,128,128]{3,2,1,0:T(8,128)(2,1)} %ker_ref.1, s32[4,1024]{1,0:T(4,128)} %bitcast.4, f32[6,4096]{1,0:T(8,128)} %coef_ref.1, s32[6,4096]{1,0:T(8,128)} %faces_ref.1, ...), custom_call_target="tpu_custom_call" | custom-call | tf_op jit(solution)/shard_map/advance/pallas_call | solution.py:246
  67.2 2.8 %hand_over.1 = (bf16[4096,256]{1,0:T(8,128)(2,1)}, bf16[2048,256]{1,0:T(8,128)(2,1)}) custom-call(bf16[4096,256]{1,0:T(8,128)(2,1)} %get-tuple-element.4.refs_0_, bf16[2048,256]{1,0:T(8,128)(2,1)} %get-tuple-element.5.refs_1_), custom_call_target="tpu_custom_call" | custom-call | tf_op jit(solution)/shard_map/hand_over/pallas_call | solution.py:297

commit v8 on v7

--- a/solution.py
+++ b/solution.py
@@ -11,6 +11,7 @@
 LANES = 128
 FACES = 6
 BLOCK = 1024
+SPARE = 16
 PARTS = 1
 UNROLL = 64
 PICKS = 8
@@ -251,10 +252,10 @@
         scratch_shapes=[
             pltpu.VMEM(dust.shape, bf16),
             pltpu.VMEM(kernels.shape, bf16),
-            pltpu.VMEM((2 * (rows + sent), LANES), f32),
-            pltpu.VMEM((2 * FACES * rows, LANES), f32),
-            pltpu.VMEM((2 * rows, LANES), f32),
-            pltpu.VMEM((export_ids.shape[1], LANES), f32),
+            pltpu.VMEM((2 * (rows + sent) + SPARE, LANES), f32),
+            pltpu.VMEM((2 * FACES * rows + SPARE, LANES), f32),
+            pltpu.VMEM((2 * rows + SPARE, LANES), f32),
+            pltpu.VMEM((export_ids.shape[1] + SPARE, LANES), f32),
             pltpu.VMEM((SPECIES, sent, LANES), bf16),
             pltpu.VMEM((SPECIES, sent, LANES), bf16),
             pltpu.VMEM((moved, width), bf16),

time: 71.2 us -> 70.4 us (0.989)
  no operation moved by 1% of the time
where the time goes in v8:
time: 70.4 us; the launch traced here: 69.7 us
  Pallas kernels  69 us (98%)
    pallas_call x1, Pallas kernels, advance(): pl.pallas_call(functools.partial(step_kernel, n_dx, n_dy), in_specs=[hbm,...  66.2 us
    pallas_call x1, Pallas kernels, hand_over(): pl.pallas_call(functools.partial(hand_over_kernel, pieces), in_specs=[hbm...  2.83 us

profile of v8, /device:TPU:1, one launch (start us, length us, event | category | flops | bytes accessed | tf_op | source)
XLA Modules:
  0.0 69.7 jit_solution(6714764918590319680)
XLA Ops:
  0.6 66.2 %advance.1 = (bf16[4096,256]{1,0:T(8,128)(2,1)}, bf16[2048,256]{1,0:T(8,128)(2,1)}) custom-call(bf16[4096,256]{1,0:T(8,128)(2,1)} %dust_ref.1, s32[32,128]{1,0:T(8,128)} %bitcast.3, bf16[8,2,128,128]{3,2,1,0:T(8,128)(2,1)} %ker_ref.1, s32[4,1024]{1,0:T(4,128)} %bitcast.4, f32[6,4096]{1,0:T(8,128)} %coef_ref.1, s32[6,4096]{1,0:T(8,128)} %faces_ref.1, ...), custom_call_target="tpu_custom_call" | custom-call | tf_op jit(solution)/shard_map/advance/pallas_call | solution.py:247
  66.8 2.8 %hand_over.1 = (bf16[4096,256]{1,0:T(8,128)(2,1)}, bf16[2048,256]{1,0:T(8,128)(2,1)}) custom-call(bf16[4096,256]{1,0:T(8,128)(2,1)} %get-tuple-element.4.refs_0_, bf16[2048,256]{1,0:T(8,128)(2,1)} %get-tuple-element.5.refs_1_), custom_call_target="tpu_custom_call" | custom-call | tf_op jit(solution)/shard_map/hand_over/pallas_call | solution.py:298
